TPU v7x, 512 devices: a whole 4x8x8 slice. The times are simulated.
512 devices in a mesh: ctx: 128 (over y, z_hi, x, core), ch: 4 (over z_lo).
Axes of the slice: x: 4, y: 8, z: 8 (z_hi: 2, z_lo: 4; z = z_hi * 4 + z_lo), core: 2. Of those that a mesh axis runs over, the one named last changes fastest.
Arguments:
- queries: bfloat16 [16384, 8192], P('ctx', 'ch'), may hold values from -6 to 6
- key_input: bfloat16 [16384, 8192], P('ctx', 'ch'), may hold values from -6 to 6
- value_input: bfloat16 [16384, 8192], P('ctx', 'ch'), may hold values from -6 to 6
- cotangent: bfloat16 [16384, 8192], P('ctx', 'ch'), may hold values from -60 to 60, as said below
- residues: float32 [512, 16], replicated, may hold values from -1 to 1
- log_rates: float32 [512, 16], replicated, may hold values from -14 to -3
- skip_gain: float32 [8192], replicated, may hold values from -1 to 1
Outputs:
- grad_query: bfloat16 [16384, 8192], P('ctx', 'ch')
- grad_key: bfloat16 [16384, 8192], P('ctx', 'ch')
- grad_value: bfloat16 [16384, 8192], P('ctx', 'ch')
- grad_residue: float32 [512, 16], replicated
- grad_lograte: float32 [512, 16], replicated
- grad_skip: float32 [8192], replicated
Inputs may be any that keep to these rules, and one draw needn't show every extreme that they name: Every row of the cotangent has its own scale.
All inputs are finite; a program needn't handle non-finite values.
Results may differ from a plain program's by a relative error of at most 0.017.
Values may be sent and summed in bfloat16 or wider, within the bound.
A program may use at most 64 MiB of HBM per device.

v0:
```python
import math

import jax
import jax.numpy as jnp
from jax import lax
from jax.sharding import PartitionSpec as P

GROUP = 16


highest = lax.Precision.HIGHEST


def split_factor(length):
    chosen = 1
    for factor in range(1, math.isqrt(length) + 1):
        if length % factor == 0:
            chosen = factor
    return chosen


def phase_table(row_count, col_count, period):
    row_index = lax.broadcasted_iota(jnp.int32, (row_count, col_count), 0)
    col_index = lax.broadcasted_iota(jnp.int32, (row_count, col_count), 1)
    angle = (row_index * col_index % period).astype(jnp.float32) * (2.0 * math.pi / period)
    return (jnp.cos(angle), jnp.sin(angle))


def contract_middle(operand, phases):
    return jnp.einsum("man,ak->mkn", operand, phases, precision=highest)


def contract_last(operand, phases):
    return jnp.einsum("mkn,nb->mkb", operand, phases, precision=highest)


def forward_transform(real_part, imag_part, inner_size, outer_size, padded):
    cos_first, sin_first = phase_table(real_part.shape[1], inner_size, inner_size)
    first_re = contract_middle(real_part, cos_first) + contract_middle(imag_part, sin_first)
    first_im = contract_middle(imag_part, cos_first) - contract_middle(real_part, sin_first)
    cos_twist, sin_twist = phase_table(inner_size, outer_size, padded)
    twist_re = first_re * cos_twist + first_im * sin_twist
    twist_im = first_im * cos_twist - first_re * sin_twist
    cos_second, sin_second = phase_table(outer_size, outer_size, outer_size)
    final_re = contract_last(twist_re, cos_second) + contract_last(twist_im, sin_second)
    final_im = contract_last(twist_im, cos_second) - contract_last(twist_re, sin_second)
    return (final_re, final_im)


def inverse_transform(real_part, imag_part, half_rows, inner_size, outer_size, padded):
    cos_second, sin_second = phase_table(outer_size, outer_size, outer_size)
    first_re = contract_last(real_part, cos_second) - contract_last(imag_part, sin_second)
    first_im = contract_last(imag_part, cos_second) + contract_last(real_part, sin_second)
    cos_twist, sin_twist = phase_table(inner_size, outer_size, padded)
    twist_re = first_re * cos_twist - first_im * sin_twist
    twist_im = first_im * cos_twist + first_re * sin_twist
    cos_first, sin_first = phase_table(inner_size, half_rows, inner_size)
    final_re = (
        contract_middle(twist_re, cos_first) - contract_middle(twist_im, sin_first)
    ) / padded
    final_im = (
        contract_middle(twist_im, cos_first) + contract_middle(twist_re, sin_first)
    ) / padded
    return (final_re, final_im)


def mirror_spectrum(spectrum):
    flipped = jnp.roll(jnp.flip(spectrum, (1, 2)), 1, axis=1)
    first_row = jnp.roll(flipped[:, :1, :], 1, axis=2)
    return jnp.concatenate([first_row, flipped[:, 1:, :]], axis=1)


def filter_spectrum(local_residues, local_rates, length, inner_size, outer_size):
    padded = 2 * length
    row_index = lax.broadcasted_iota(jnp.int32, (inner_size, outer_size), 0)
    col_index = lax.broadcasted_iota(jnp.int32, (inner_size, outer_size), 1)
    freq_index = row_index + inner_size * col_index
    theta = freq_index.astype(jnp.float32) * (2.0 * math.pi / padded)
    half_angle = freq_index.astype(jnp.float32) * (math.pi / padded)
    parity = (freq_index % 2).astype(jnp.float32)
    rates = local_rates[:, :, None, None]
    decay_one = jnp.exp(-rates)
    tail_keep = jnp.exp(-rates * length)
    tail_loss = -jnp.expm1(-rates * length)
    numer = local_residues[:, :, None, None] * (
        (1.0 - parity) * tail_loss + parity * (1.0 + tail_keep)
    )
    denom_re = -jnp.expm1(-rates) + 2.0 * decay_one * jnp.sin(half_angle) ** 2
    denom_im = decay_one * jnp.sin(theta)
    weight = numer / (denom_re * denom_re + denom_im * denom_im)
    return (jnp.sum(weight * denom_re, axis=1), -jnp.sum(weight * denom_im, axis=1))


def product(left, right):
    return (left.astype(jnp.float32) * right.astype(jnp.float32)).astype(jnp.bfloat16)


def local(queries, key_input, value_input, cotangent, residues, log_rates, skip_gain):
    tok_rows, shard_width = queries.shape
    ctx_parts = lax.axis_size("ctx")
    per_dev = shard_width // ctx_parts
    length = tok_rows * ctx_parts
    padded = 2 * length
    shard_groups = residues.shape[0] // lax.axis_size("ch")
    ctx_index = lax.axis_index("ctx")
    ch_index = lax.axis_index("ch")
    outer_size = split_factor(length)
    inner_size = padded // outer_size
    half_rows = length // outer_size
    local_groups = per_dev // GROUP
    first_group = ch_index * shard_groups + ctx_index * local_groups
    local_residues = lax.dynamic_slice_in_dim(residues, first_group, local_groups, 0)
    local_logs = lax.dynamic_slice_in_dim(log_rates, first_group, local_groups, 0)
    local_rates = jnp.exp(local_logs)
    local_skip = lax.dynamic_slice_in_dim(
        skip_gain, ch_index * shard_width + ctx_index * per_dev, per_dev, 0
    )
    spec_re, spec_im = filter_spectrum(local_residues, local_rates, length, inner_size, outer_size)

    def by_block(tensor):
        return tensor.reshape(tok_rows, ctx_parts, per_dev)

    def by_channel(tensor):
        return tensor.reshape(length, per_dev)

    def by_owner(tensor):
        return tensor.reshape(ctx_parts, tok_rows, per_dev)

    def by_rows(tensor):
        return tensor.reshape(tok_rows, shard_width)

    query_ch, key_ch, value_ch, cotan_ch = (
        lax.all_to_all(by_block(queries), "ctx", split_axis=1, concat_axis=0, tiled=True),
        lax.all_to_all(by_block(key_input), "ctx", split_axis=1, concat_axis=0, tiled=True),
        lax.all_to_all(by_block(value_input), "ctx", split_axis=1, concat_axis=0, tiled=True),
        lax.all_to_all(by_block(cotangent), "ctx", split_axis=1, concat_axis=0, tiled=True),
    )
    query_ch = by_channel(query_ch)
    key_ch = by_channel(key_ch)
    value_ch = by_channel(value_ch)
    cotan_ch = by_channel(cotan_ch)
    gated_ch = product(key_ch, value_ch)
    dgate_ch = product(cotan_ch, query_ch)
    gated_rows = gated_ch.astype(jnp.float32).T.reshape(per_dev, half_rows, outer_size)
    dgate_rows = dgate_ch.astype(jnp.float32).T.reshape(per_dev, half_rows, outer_size)
    packed_re, packed_im = forward_transform(gated_rows, dgate_rows, inner_size, outer_size, padded)
    mirror_re = mirror_spectrum(packed_re)
    mirror_im = mirror_spectrum(packed_im)
    shape_four = (local_groups, GROUP, inner_size, outer_size)
    gate_re = (0.5 * (packed_re + mirror_re)).reshape(shape_four)
    gate_im = (0.5 * (packed_im - mirror_im)).reshape(shape_four)
    back_re = (0.5 * (packed_im + mirror_im)).reshape(shape_four)
    back_im = (0.5 * (mirror_re - packed_re)).reshape(shape_four)
    filt_re = spec_re[:, None]
    filt_im = spec_im[:, None]
    fwd_re = filt_re * gate_re - filt_im * gate_im
    fwd_im = filt_re * gate_im + filt_im * gate_re
    adj_re = filt_re * back_re + filt_im * back_im
    adj_im = filt_re * back_im - filt_im * back_re
    joint_re = (fwd_re - adj_im).reshape(per_dev, inner_size, outer_size)
    joint_im = (fwd_im + adj_re).reshape(per_dev, inner_size, outer_size)
    conv_z, conv_flow = inverse_transform(
        joint_re, joint_im, half_rows, inner_size, outer_size, padded
    )
    conv_z = conv_z.reshape(per_dev, length).T
    conv_flow = conv_flow.reshape(per_dev, length).T
    hidden_z = (local_skip[None, :] * gated_ch.astype(jnp.float32) + conv_z).astype(jnp.bfloat16)
    flow = (local_skip[None, :] * dgate_ch.astype(jnp.float32) + conv_flow).astype(jnp.bfloat16)
    cross_re = jnp.sum(gate_re * back_re + gate_im * back_im, axis=1)
    cross_im = jnp.sum(gate_re * back_im - gate_im * back_re, axis=1)
    filter_grad = inverse_transform(cross_re, cross_im, half_rows, inner_size, outer_size, padded)[
        0
    ]
    filter_grad = filter_grad.reshape(local_groups, length)
    positions = jnp.arange(length).astype(jnp.float32)
    decays = jnp.exp(-local_rates[:, :, None] * positions[None, None, :])
    grad_res = jnp.einsum("gpl,gl->gp", decays, filter_grad, precision=highest) / length
    moment = jnp.einsum(
        "gpl,gl->gp", decays * positions[None, None, :], filter_grad, precision=highest
    )
    grad_log = -local_rates * local_residues * moment / math.sqrt(length)
    query_grad_ch = product(cotan_ch, hidden_z)
    key_grad_ch = product(flow, value_ch)
    value_grad_ch = product(flow, key_ch)
    grad_query, grad_key, grad_value = (
        lax.all_to_all(by_owner(query_grad_ch), "ctx", split_axis=0, concat_axis=2, tiled=True),
        lax.all_to_all(by_owner(key_grad_ch), "ctx", split_axis=0, concat_axis=2, tiled=True),
        lax.all_to_all(by_owner(value_grad_ch), "ctx", split_axis=0, concat_axis=2, tiled=True),
    )
    grad_query = by_rows(grad_query)
    grad_key = by_rows(grad_key)
    grad_value = by_rows(grad_value)
    seq_terms = jnp.sum(
        product(cotangent, queries).astype(jnp.float32)
        * product(key_input, value_input).astype(jnp.float32),
        axis=0,
    )
    skip_total = lax.psum(seq_terms, "ctx") / math.sqrt(length)
    res_shard, log_shard = (
        lax.all_gather(grad_res, "ctx", axis=0, tiled=True),
        lax.all_gather(grad_log, "ctx", axis=0, tiled=True),
    )
    grad_residue, grad_lograte, grad_skip = (
        lax.all_gather(res_shard, "ch", axis=0, tiled=True),
        lax.all_gather(log_shard, "ch", axis=0, tiled=True),
        lax.all_gather(skip_total, "ch", axis=0, tiled=True),
    )
    return (grad_query, grad_key, grad_value, grad_residue, grad_lograte, grad_skip)


def solution(mesh):
    placed = (P("ctx", "ch"), P("ctx", "ch"), P("ctx", "ch"), P("ctx", "ch"), P(), P(), P())
    return jax.shard_map(
        local,
        mesh=mesh,
        in_specs=placed,
        out_specs=(P("ctx", "ch"), P("ctx", "ch"), P("ctx", "ch"), P(), P(), P()),
        check_vma=False,
    )
```

profile of v0, /device:TPU:1, one launch (start us, length us, event | category | flops | bytes accessed | tf_op | source)
XLA Modules:
  0.0 1359.4 jit_solution(5177493851116107434)
XLA Ops:
  0.7 2.1 copy.86
  2.8 20.8 %all-to-all-start = ((bf16[128,128,16]{0,2,1:T(8,128)(2,1)}), bf16[128,128,16]{0,2,1:T(8,128)(2,1)S(1)}, u32[]{:S(2)}, u32[]{:S(2)}) async-start(bf16[128,128,16]{0,2,1:T(8,128)(2,1)} %bitcast), calls=%async_computation | async-start | bytes 1048576 | tf_op jit(solution)/shard_map/all_to_all | solution.py:136
  23.6 1.0 copy.88
  24.6 22.0 %all-to-all-done = bf16[128,128,16]{0,2,1:T(8,128)(2,1)S(1)} async-done(((bf16[128,128,16]{0,2,1:T(8,128)(2,1)}), bf16[128,128,16]{0,2,1:T(8,128)(2,1)S(1)}, u32[]{:S(2)}, u32[]{:S(2)}) %all-to-all-start) | async-done | bytes 524320 | tf_op jit(solution)/shard_map/all_to_all | solution.py:136
  46.7 5.9 all-to-all-start.1
  52.6 1.0 copy.90
  55.2 20.4 %all-to-all-done.1 = bf16[128,128,16]{0,2,1:T(8,128)(2,1)S(1)} async-done(((bf16[128,128,16]{0,2,1:T(8,128)(2,1)}), bf16[128,128,16]{0,2,1:T(8,128)(2,1)S(1)}, u32[]{:S(2)}, u32[]{:S(2)}) %all-to-all-start.1) | async-done | bytes 524320 | tf_op jit(solution)/shard_map/all_to_all | solution.py:134
  75.6 5.9 all-to-all-start.2
  82.1 1.0 copy.92
  83.1 0.9 broadcast_subtract_fusion
  84.1 1.3 multiply_reduce_fusion
  86.0 18.6 %all-to-all-done.2 = bf16[128,128,16]{0,2,1:T(8,128)(2,1)S(1)} async-done(((bf16[128,128,16]{0,2,1:T(8,128)(2,1)}), bf16[128,128,16]{0,2,1:T(8,128)(2,1)S(1)}, u32[]{:S(2)}, u32[]{:S(2)}) %all-to-all-start.2) | async-done | bytes 524320 | tf_op jit(solution)/shard_map/all_to_all | solution.py:135
  104.6 6.9 all-to-all-start.3
  112.1 1.3 dynamic_slice.9
  114.9 1.0 copy-done.10
  116.3 17.6 %all-to-all-done.3 = bf16[128,128,16]{0,2,1:T(8,128)(2,1)} async-done(((bf16[128,128,16]{0,2,1:T(8,128)(2,1)}), bf16[128,128,16]{0,2,1:T(8,128)(2,1)}, u32[]{:S(2)}, u32[]{:S(2)}) %all-to-all-start.3) | async-done | bytes 524320 | tf_op jit(solution)/shard_map/all_to_all | solution.py:133
  133.8 1.1 convert_bitcast_fusion
  135.3 2.3 fusion.33
  137.7 1.4 fusion.61
  139.3 1.4 fusion.63
  140.7 1.6 convolution_subtract_fusion
  142.2 1.6 convolution_add_fusion
  143.8 2.4 fusion.5
  146.2 2.2 fusion.11
  148.5 1.6 slice.60
  150.2 2.2 fusion.3
  152.4 2.3 fusion.14
  154.7 1.8 slice.63
  156.7 17.9 %slice.52 = f32[16,255,128]{2,1,0:T(8,128)} reverse(f32[16,255,128]{2,1,0:T(8,128)} %slice.60), dimensions={1,2} | reverse | bytes 4177920 | tf_op jit(solution)/shard_map/jit(_roll_static)/slice | solution.py:68
  175.3 17.9 %slice.57 = f32[16,255,128]{2,1,0:T(8,128)} reverse(f32[16,255,128]{2,1,0:T(8,128)} %slice.63), dimensions={1,2} | reverse | bytes 4177920 | tf_op jit(solution)/shard_map/jit(_roll_static)/slice | solution.py:68
  194.0 4.6 add_reduce_fusion
  198.6 1.2 subtract_subtract_fusion
  199.8 2.1 fusion.94
  202.0 2.1 fusion.96
  204.1 2.1 convolution_add_fusion.1
  206.3 2.1 convolution_subtract_fusion.1
  208.4 2.0 fusion.41
  210.4 2.4 fusion.42
  212.8 2.0 fusion.21
  214.9 2.0 fusion.22
  216.9 3.4 fusion.44
  220.4 1.4 copy_bitcast_fusion.1
  221.8 6.3 all-to-all-start.5
  228.2 1.7 multiply_exponential_fusion
  229.8 1.3 dynamic-slice
  231.8 0.9 copy.157
  232.6 18.4 %all-to-all-done.5 = bf16[128,128,16]{1,2,0:T(8,128)(2,1)S(1)} async-done(((bf16[128,128,16]{1,2,0:T(8,128)(2,1)}), bf16[128,128,16]{1,2,0:T(8,128)(2,1)S(1)}, u32[]{:S(2)}, u32[]{:S(2)}) %all-to-all-start.5) | async-done | bytes 524320 | tf_op jit(solution)/shard_map/all_to_all | solution.py:187
  251.1 6.0 all-to-all-start.4
  257.1 1.6 multiply_reduce_fusion.1
  258.7 0.9 copy.156
  261.7 18.5 %all-to-all-done.4 = bf16[128,128,16]{1,2,0:T(8,128)(2,1)S(1)} async-done(((bf16[128,128,16]{1,2,0:T(8,128)(2,1)}), bf16[128,128,16]{1,2,0:T(8,128)(2,1)S(1)}, u32[]{:S(2)}, u32[]{:S(2)}) %all-to-all-start.4) | async-done | bytes 524320 | tf_op jit(solution)/shard_map/all_to_all | solution.py:186
  280.1 6.2 all-to-all-start.6
  286.4 1.3 fusion.70
  287.7 1.3 fusion.23
  289.0 1.7 fusion.24
  290.9 798.8 %all-reduce.1 = (f32[2048]{0:T(1024)S(1)}, f32[2048]{0:T(1024)S(1)}) all-reduce(f32[2048]{0:T(1024)S(1)} %dynamic-update-slice, f32[2048]{0:T(1024)S(1)} %multiply_reduce_fusion.1), channel_id=2, replica_groups=mesh['ctx'=128,'ch'=4] {'ctx'}, use_global_device_ids=true, to_apply=%add | all-reduce | flops 4096 | bytes 32768
  1089.8 11.2 all_gather.16
  1101.7 10.5 all_gather.19
  1112.2 1.5 fusion.26
  1113.7 229.0 %all-gather.1 = f32[128,1,16]{2,1,0:T(1,128)S(1)} all-gather(f32[1,1,16]{2,1,0:T(1,128)S(1)} %fusion.26), channel_id=1, replica_groups=mesh['ctx'=128,'ch'=4] {'ctx'}, dimensions={0}, use_global_device_ids=true | all-gather | bytes 8256 | tf_op jit(solution)/shard_map/all_gather | solution.py:201
  1342.6 12.2 all_gather.18
  1355.5 1.0 copy.104
  1356.5 1.0 copy.103
  1357.5 1.0 copy.105
  (91 shorter events, 12.1 us)
Async XLA Ops:
  0.6 23.0 %copy-start.11 = (bf16[128,2048]{1,0:T(8,128)(2,1)S(1)}, bf16[128,2048]{1,0:T(8,128)(2,1)}, u32[]{:S(2)}) copy-start(bf16[128,2048]{1,0:T(8,128)(2,1)} %param.8) | copy-start | bytes 1572868
  0.6 51.9 %copy-start.15 = (bf16[128,2048]{1,0:T(8,128)(2,1)S(1)}, bf16[128,2048]{1,0:T(8,128)(2,1)}, u32[]{:S(2)}) copy-start(bf16[128,2048]{1,0:T(8,128)(2,1)} %param.9) | copy-start | bytes 1572868
  2.8 43.9 %all-to-all-start = ((bf16[128,128,16]{0,2,1:T(8,128)(2,1)}), bf16[128,128,16]{0,2,1:T(8,128)(2,1)S(1)}, u32[]{:S(2)}, u32[]{:S(2)}) async-start(bf16[128,128,16]{0,2,1:T(8,128)(2,1)} %bitcast), calls=%async_computation | async-start | bytes 1048576 | tf_op jit(solution)/shard_map/all_to_all | solution.py:136
  23.6 58.4 %copy-start.13 = (bf16[128,2048]{1,0:T(8,128)(2,1)S(1)}, bf16[128,2048]{1,0:T(8,128)(2,1)}, u32[]{:S(2)}) copy-start(bf16[128,2048]{1,0:T(8,128)(2,1)} %param.7) | copy-start | bytes 1572868
  46.7 28.9 %all-to-all-start.1 = ((bf16[128,128,16]{0,2,1:T(8,128)(2,1)}), bf16[128,128,16]{0,2,1:T(8,128)(2,1)S(1)}, u32[]{:S(2)}, u32[]{:S(2)}) async-start(bf16[128,128,16]{0,2,1:T(8,128)(2,1)} %bitcast.3), calls=%async_computation.1 | async-start | bytes 1048576 | tf_op jit(solution)/shard_map/all_to_all | solution.py:134
  54.5 50.1 %copy-start.23 = (f32[1,16]{1,0:T(1,128)}, f32[1,16]{1,0:T(1,128)S(1)}, u32[]{:S(2)}) copy-start(f32[1,16]{1,0:T(1,128)S(1)} %copy.117) | copy-start | bytes 196
  75.6 28.9 %all-to-all-start.2 = ((bf16[128,128,16]{0,2,1:T(8,128)(2,1)}), bf16[128,128,16]{0,2,1:T(8,128)(2,1)S(1)}, u32[]{:S(2)}, u32[]{:S(2)}) async-start(bf16[128,128,16]{0,2,1:T(8,128)(2,1)} %bitcast.6), calls=%async_computation.2 | async-start | bytes 1048576 | tf_op jit(solution)/shard_map/all_to_all | solution.py:135
  83.1 30.2 %copy-start.21 = (f32[1,16]{1,0:T(1,128)}, f32[1,16]{1,0:T(1,128)S(1)}, u32[]{:S(2)}) copy-start(f32[1,16]{1,0:T(1,128)S(1)} %copy.118) | copy-start | bytes 196
  104.6 9.4 copy-start.9
  104.6 29.3 %all-to-all-start.3 = ((bf16[128,128,16]{0,2,1:T(8,128)(2,1)}), bf16[128,128,16]{0,2,1:T(8,128)(2,1)}, u32[]{:S(2)}, u32[]{:S(2)}) async-start(bf16[128,128,16]{0,2,1:T(8,128)(2,1)} %bitcast.13), calls=%async_computation.3 | async-start | bytes 1048576 | tf_op jit(solution)/shard_map/all_to_all | solution.py:133
  114.4 20.9 %copy-start.1 = (f32[128,128,1,16]{1,0,3,2:T(8,128)}, f32[128,128,1,16]{1,0,3,2:T(8,128)S(1)}, u32[]{:S(2)}) copy-start(f32[128,128,1,16]{1,0,3,2:T(8,128)S(1)} %copy.87) | copy-start | bytes 3145732
  114.4 1.4 copy-start.10
  115.9 19.5 %copy-start.3 = (f32[128,128,1,16]{1,0,3,2:T(8,128)}, f32[128,128,1,16]{1,0,3,2:T(8,128)S(1)}, u32[]{:S(2)}) copy-start(f32[128,128,1,16]{1,0,3,2:T(8,128)S(1)} %copy.89) | copy-start | bytes 3145732
  137.6 1.5 copy-start.5
  137.6 1.6 copy-start.7
  154.6 2.0 copy-start
  194.0 4.6 copy-start.18
  194.0 4.6 copy-start.19
  214.8 2.1 copy-start.2
  214.8 2.1 copy-start.4
  214.8 2.1 copy-start.6
  214.8 2.1 copy-start.8
  214.8 2.1 copy-start.26
  220.4 7.8 copy-start.20
  220.4 7.8 copy-start.25
  221.8 35.3 %copy-start.12 = (bf16[128,2048]{1,0:T(8,128)(2,1)S(1)}, bf16[128,2048]{1,0:T(8,128)(2,1)}, u32[]{:S(2)}) copy-start(bf16[128,2048]{1,0:T(8,128)(2,1)} %param.8) | copy-start | bytes 1572868
  221.8 35.3 %copy-start.14 = (bf16[128,2048]{1,0:T(8,128)(2,1)S(1)}, bf16[128,2048]{1,0:T(8,128)(2,1)}, u32[]{:S(2)}) copy-start(bf16[128,2048]{1,0:T(8,128)(2,1)} %param.7) | copy-start | bytes 1572868
  221.8 29.2 %all-to-all-start.5 = ((bf16[128,128,16]{1,2,0:T(8,128)(2,1)}), bf16[128,128,16]{1,2,0:T(8,128)(2,1)S(1)}, u32[]{:S(2)}, u32[]{:S(2)}) async-start(bf16[128,128,16]{1,2,0:T(8,128)(2,1)} %copy_bitcast_fusion.1), calls=%async_computation.5 | async-start | bytes 1048576 | tf_op jit(solution)/shard_map/all_to_all | solution.py:187
  251.1 9.0 copy-start.17
  251.1 29.1 %all-to-all-start.4 = ((bf16[128,128,16]{1,2,0:T(8,128)(2,1)}), bf16[128,128,16]{1,2,0:T(8,128)(2,1)S(1)}, u32[]{:S(2)}, u32[]{:S(2)}) async-start(bf16[128,128,16]{1,2,0:T(8,128)(2,1)} %bitcast.230), calls=%async_computation.4 | async-start | bytes 1048576 | tf_op jit(solution)/shard_map/all_to_all | solution.py:186
  257.1 1.6 copy-start.16
  280.1 1077.4 %all-to-all-start.6 = ((bf16[128,128,16]{1,2,0:T(8,128)(2,1)}), bf16[128,128,16]{1,2,0:T(8,128)(2,1)S(1)}, u32[]{:S(2)}, u32[]{:S(2)}) async-start(bf16[128,128,16]{1,2,0:T(8,128)(2,1)} %bitcast.229), calls=%async_computation.6 | async-start | bytes 1048576 | tf_op jit(solution)/shard_map/all_to_all | solution.py:188
  286.3 825.8 %copy-start.22 = (f32[1,16]{1,0:T(1,128)S(1)}, f32[1,16]{1,0:T(1,128)}, u32[]{:S(2)}) copy-start(f32[1,16]{1,0:T(1,128)} %copy-done.21) | copy-start | bytes 196
  286.4 825.8 %copy-start.24 = (f32[1,16]{1,0:T(1,128)S(1)}, f32[1,16]{1,0:T(1,128)}, u32[]{:S(2)}) copy-start(f32[1,16]{1,0:T(1,128)} %copy-done.23) | copy-start | bytes 196
where the time goes:
time: 1370 us; the launch traced here: 1360 us
  blocking collectives  1060 us (77%)
  waiting for transfers between devices  115 us (8%)
  local copies, waits for them, and re-layouts  59.4 us (4%)
  starting transfers between devices  58 us (4%)
  matrix products  39.8 us (3%)
  other arithmetic  22.9 us (2%)
    unnamed x1, blocking collectives  799 us
    all_gather x1, blocking collectives, local(): lax.all_gather(grad_log, 'ctx', axis=0, tiled=True)  229 us
    slice x4, local copies, waits for them, and re-layouts, mirror_spectrum(): flipped = jnp.roll(jnp.flip(spectrum, (1, 2)), 1, axis=1)  39.2 us
  transfers between devices with their start and end apart: 7, of which 6 were waited for; matrix products, arithmetic and copies ran while one was open for 2% of the time, Pallas kernels for 0%

commit v1 on v0

v1 whole, which is shorter than its diff:
```python
import functools
import math

import jax
import jax.numpy as jnp
from jax import lax
from jax.experimental import pallas as pl
from jax.experimental.pallas import tpu as pltpu
from jax.sharding import PartitionSpec as P

GROUP = 16
POLES = 16
OWN = 8
BLK = 256
TOK = 128

MESH = pl.DeviceIdType.MESH
F32 = jnp.float32
BF16 = jnp.bfloat16
HIGHEST = lax.Precision.HIGHEST


def iota(shape, dim):
    return lax.broadcasted_iota(jnp.int32, shape, dim)


def dot(a, b, dims=((1,), (0,)), precision=None):
    return lax.dot_general(
        a, b, (dims, ((), ())), precision=precision, preferred_element_type=F32
    )


def comm_kernel(
    nsb, nch,
    q_ref, k_ref, v_ref, c_ref, res_ref, log_ref, skip_ref,
    z_ref, f_ref, g_ref,
    x_s, d_s, ed_s, el_s, ed2_s, el2_s, h_s, hr_s, zl_s, fl_s,
    p1s, p1r, p2s, p2r, p3s, p3r, pbs, pbr, p4s, p4r, p5s, p5r,
    s1, r1, s2, r2, s3, r3, sb_, rb_, s4, r4, s5, r5,
):
    ctx = lax.axis_index("ctx")
    ch = lax.axis_index("ch")
    own = ctx % OWN
    sup = ctx // OWN

    barrier = pltpu.get_barrier_semaphore()

    def greet(ctx_to, ch_to):
        pl.semaphore_signal(barrier, inc=1, device_id=(ctx_to, ch_to), device_id_type=MESH)

    @pl.loop(1, OWN)
    def _(j):
        greet(sup * OWN + (own + j) % OWN, ch)

    @pl.loop(1, nsb)
    def _(j):
        greet(((sup + j) % nsb) * OWN + own, ch)

    @pl.loop(1, nch)
    def _(i):
        @pl.loop(0, OWN)
        def _(j):
            greet(sup * OWN + j, (ch + i) % nch)

    lane_t = iota((GROUP, TOK), 1).astype(F32)
    same_group = (iota((BLK, BLK), 0) % 16) == (iota((BLK, BLK), 1) // 16)
    pick_pole = ((iota((POLES, BLK), 1) // 16) == iota((POLES, BLK), 0)).astype(BF16)
    spread_pole = ((iota((BLK, POLES), 0) // 16) == iota((BLK, POLES), 1)).astype(BF16)

    @pl.loop(0, OWN)
    def _(i):
        rows = pl.ds(pl.multiple_of(ch * 128 + i * 16, 16), 16)
        cols = pl.ds(pl.multiple_of(i * BLK, BLK), BLK)
        lam = jnp.exp(log_ref[rows, :])
        res = res_ref[rows, :]
        taps = jnp.zeros((GROUP, TOK), F32)
        back = jnp.zeros((GROUP, TOK), F32)
        for p in range(POLES):
            lam_p = lam[:, p : p + 1]
            res_p = res[:, p : p + 1]
            ed = jnp.exp(-lam_p * lane_t)
            el = jnp.exp(-lam_p * (TOK - 1.0 - lane_t))
            at = pl.ds(p * 16, 16)
            ed_s[i, at, :] = ed.astype(BF16)
            el_s[i, at, :] = el.astype(BF16)
            ed2_s[i, at, :] = (ed * (lane_t + 1.0)).astype(BF16)
            el2_s[i, at, :] = (el * (TOK - 1.0 - lane_t)).astype(BF16)
            taps = taps + res_p * ed
            back = back + (res_p * jnp.exp(-lam_p)) * el
        h_s[i] = taps
        hr_s[i] = jnp.where(lane_t == 0.0, taps, back)
        x = (k_ref[:, cols].astype(F32) * v_ref[:, cols].astype(F32)).astype(BF16)
        d = (c_ref[:, cols].astype(F32) * q_ref[:, cols].astype(F32)).astype(BF16)
        x_s[:, cols] = x
        d_s[:, cols] = d
        pbs[i, 2:3, :] = jnp.sum(x.astype(F32) * d.astype(F32), axis=0, keepdims=True)
        for n, (table, val) in enumerate(((el_s, x), (ed_s, d), (el2_s, x), (ed2_s, d))):
            full = dot(table[i], val)
            full = jnp.where(same_group, full, 0.0).astype(BF16)
            p1s[i, n] = dot(pick_pole, full).astype(BF16)

    pl.semaphore_wait(barrier, (OWN - 1) + (nsb - 1) + (nch - 1) * OWN)

    def to_own(j, src, dst, send, recv):
        other = (own + j) % OWN
        return pltpu.make_async_remote_copy(
            src_ref=src.at[other], dst_ref=dst.at[own], send_sem=send.at[other], recv_sem=recv.at[own],
            device_id=(sup * OWN + other, ch), device_id_type=MESH,
        )

    def from_own(j, src, dst, send, recv):
        other = (own + j) % OWN
        return pltpu.make_async_remote_copy(
            src_ref=src.at[other], dst_ref=dst.at[other], send_sem=send.at[other], recv_sem=recv.at[other],
            device_id=(sup * OWN + other, ch), device_id_type=MESH,
        )

    def send_own(*args):
        @pl.loop(1, OWN)
        def _(j):
            to_own(j, *args).start()

    def wait_own(*args):
        @pl.loop(1, OWN)
        def _(j):
            from_own(j, *args).wait_recv()

    def sent_own(*args):
        @pl.loop(1, OWN)
        def _(j):
            from_own(j, *args).wait_send()

    send_own(p1s, p1r, s1, r1)
    p1r[own] = p1s[own]
    p2r[sup] = jnp.zeros((POLES, BLK), BF16)

    row_t = iota((TOK, TOK), 0)
    col_t = iota((TOK, TOK), 1)
    lane_group = iota((TOK, BLK), 1) // 16

    @pl.loop(0, OWN)
    def _(i):
        cols = pl.ds(pl.multiple_of(i * BLK, BLK), BLK)
        x = x_s[:, cols]
        acc = jnp.zeros((TOK, BLK), F32)
        hr = hr_s[i]
        for g in range(16):
            wide = jnp.broadcast_to(hr[g : g + 1, :], (TOK, TOK))
            mat = pltpu.roll(wide, 0, 1, stride=1, stride_axis=0)
            mat = jnp.where(col_t <= row_t, mat, 0.0).astype(BF16)
            acc = jnp.where(lane_group == g, dot(mat, x), acc)
        zl_s[:, cols] = acc

    rows = pl.ds(pl.multiple_of(ch * 128 + own * 16, 16), 16)
    lam_own = jnp.exp(log_ref[rows, :])
    res_own = res_ref[rows, :]
    to_chan = ((iota((16, BLK), 1) // 16) == iota((16, BLK), 0)).astype(F32)
    lam_pc = dot(lam_own, to_chan, ((0,), (0,)), HIGHEST)
    res_pc = dot(res_own, to_chan, ((0,), (0,)), HIGHEST)
    w = jnp.exp(-float(TOK) * lam_pc)
    e1 = jnp.exp(-lam_pc)
    re1 = res_pc * e1

    wait_own(p1s, p1r, s1, r1)
    sum_l = jnp.zeros((POLES, BLK), F32)
    sum_d = jnp.zeros((POLES, BLK), F32)
    for b in range(OWN):
        sum_l = w * sum_l + p1r[b, 0].astype(F32)
        sum_d = w * sum_d + p1r[OWN - 1 - b, 1].astype(F32)
    p2s[0] = sum_l.astype(BF16)
    p2s[1] = sum_d.astype(BF16)

    def sup_copy(j, slot):
        other = (sup + j) % nsb
        later = (other > sup).astype(jnp.int32)
        return pltpu.make_async_remote_copy(
            src_ref=p2s.at[1 - later], dst_ref=p2r.at[slot], send_sem=s2.at[other], recv_sem=r2.at[slot],
            device_id=(other * OWN + own, ch), device_id_type=MESH,
        )

    @pl.loop(1, nsb)
    def _(j):
        sup_copy(j, sup).start()

    lane_row = iota((16, BLK), 1)
    diag = (lane_row % 16) == iota((16, BLK), 0)
    flip = (row_t == TOK - 1 - col_t).astype(BF16)

    @pl.loop(0, OWN)
    def _(i):
        cols = pl.ds(pl.multiple_of(i * BLK, BLK), BLK)
        x = dot(flip, x_s[:, cols]).astype(BF16)
        d = d_s[:, cols]
        sums = []
        for g in range(16):
            dm = jnp.where(lane_group == g, d, jnp.zeros_like(d))
            corr = dot(x, dm, ((1,), (1,)))
            corr = jnp.where(col_t >= TOK - 1 - row_t, corr, 0.0)
            corr = pltpu.roll(corr, 1, 1, stride=1, stride_axis=0)
            sums.append(jnp.sum(corr, axis=0, keepdims=True))
        fg = jnp.concatenate(sums, axis=0)
        hi = fg.astype(BF16)
        lo = (fg - hi.astype(F32)).astype(BF16)
        both = jnp.concatenate([hi, lo], axis=0)
        r_in = dot(both, ed_s[i], ((1,), (1,)))
        m_in = dot(both, ed2_s[i], ((1,), (1,)))
        r_in = r_in[:16] + r_in[16:]
        m_in = m_in[:16] + m_in[16:] - r_in
        pbs[i, 0:1, :] = jnp.sum(jnp.where(diag, r_in, 0.0), axis=0, keepdims=True)
        pbs[i, 1:2, :] = jnp.sum(jnp.where(diag, m_in, 0.0), axis=0, keepdims=True)
        pbs[i, 3:4, :] = jnp.zeros((1, BLK), F32)

    send_own(pbs, pbr, sb_, rb_)
    pbr[own] = pbs[own]

    @pl.loop(0, OWN)
    def _(i):
        cols = pl.ds(pl.multiple_of(i * BLK, BLK), BLK)
        d = d_s[:, cols]
        acc = jnp.zeros((TOK, BLK), F32)
        h = h_s[i]
        for g in range(16):
            wide = jnp.broadcast_to(h[g : g + 1, :], (TOK, TOK))
            mat = pltpu.roll(wide, 0, 1, stride=1, stride_axis=0)
            mat = jnp.where(col_t >= row_t, mat, 0.0).astype(BF16)
            acc = jnp.where(lane_group == g, dot(mat, d), acc)
        fl_s[:, cols] = acc

    @pl.loop(1, nsb)
    def _(j):
        sup_copy(j, (sup + j) % nsb).wait_recv()

    in_s = jnp.zeros((POLES, BLK), F32)
    in_f = jnp.zeros((POLES, BLK), F32)
    for b in range(nsb):
        gap = jnp.maximum(jnp.abs(sup - b) - 1, 0).astype(F32) * float(TOK * OWN)
        term = jnp.exp(-lam_pc * gap) * p2r[b].astype(F32)
        in_s = in_s + jnp.where(b < sup, term, 0.0)
        in_f = in_f + jnp.where(b > sup, term, 0.0)
    carry_s = []
    for b in range(OWN):
        carry_s.append(in_s)
        p3s[b, 0] = (re1 * in_s).astype(BF16)
        in_s = w * in_s + p1r[b, 0].astype(F32)
    r_sum = jnp.zeros((POLES, BLK), F32)
    m_sum = jnp.zeros((POLES, BLK), F32)
    for b in reversed(range(OWN)):
        p3s[b, 1] = (re1 * in_f).astype(BF16)
        d_b = p1r[b, 1].astype(F32)
        r_sum = r_sum + d_b * carry_s[b]
        m_sum = (
            m_sum
            + p1r[b, 3].astype(F32) * carry_s[b]
            + p1r[b, 2].astype(F32) * in_f
            + (float(TOK) * w) * (carry_s[b] * in_f)
        )
        in_f = w * in_f + d_b
    send_own(p3s, p3r, s3, r3)
    p3r[own] = p3s[own]

    chan_group = ((iota((BLK, BLK), 0) // 16) == (iota((BLK, BLK), 1) % 16)).astype(F32)
    pole_row = (iota((POLES, BLK), 1) // 16) == iota((POLES, BLK), 0)
    sums = dot(jnp.concatenate([r_sum * e1, m_sum * e1], axis=0), chan_group, precision=HIGHEST)
    r_row = jnp.sum(jnp.where(pole_row, sums[:POLES], 0.0), axis=0, keepdims=True)
    m_row = jnp.sum(jnp.where(pole_row, sums[POLES:], 0.0), axis=0, keepdims=True)
    wait_own(pbs, pbr, sb_, rb_)
    part = pbr[0]
    for b in range(1, OWN):
        part = part + pbr[b]
    p4s[0:1, :] = part[0:1] + r_row
    p4s[1:2, :] = part[1:2] + m_row
    p4s[2:4, :] = part[2:4]

    def grad_copy(j, slot):
        other = (sup + j) % nsb
        return pltpu.make_async_remote_copy(
            src_ref=p4s, dst_ref=p4r.at[slot], send_sem=s4.at[other], recv_sem=r4.at[slot],
            device_id=(other * OWN + own, ch), device_id_type=MESH,
        )

    @pl.loop(1, nsb)
    def _(j):
        grad_copy(j, sup).start()

    p4r[sup] = p4s[...]

    wait_own(p3s, p3r, s3, r3)

    @pl.loop(0, OWN)
    def _(i):
        cols = pl.ds(pl.multiple_of(i * BLK, BLK), BLK)
        skip = skip_ref[:, pl.ds(pl.multiple_of(ch * (OWN * BLK) + i * BLK, BLK), BLK)]
        for n, (table, src, loc, out) in enumerate(
            ((ed_s, x_s, zl_s, z_ref), (el_s, d_s, fl_s, f_ref))
        ):
            wide = dot(spread_pole, p3r[i, n])
            wide = jnp.where(same_group, wide, 0.0).astype(BF16)
            corr = dot(table[i], wide, ((0,), (0,)))
            out[:, cols] = (skip * src[:, cols].astype(F32) + (loc[:, cols] + corr)).astype(BF16)

    to_pole = ((iota((POLES, BLK), 1) // 16) == iota((POLES, BLK), 0)).astype(F32)
    scale = dot(-lam_own * res_own, to_pole, precision=HIGHEST)
    scale_row = jnp.sum(jnp.where(diag, scale, 0.0), axis=0, keepdims=True)
    length = float(TOK * OWN * nsb)

    @pl.loop(1, nsb)
    def _(j):
        grad_copy(j, (sup + j) % nsb).wait_recv()

    total = p4r[0]
    for b in range(1, nsb):
        total = total + p4r[b]
    p5s[0:1, :] = total[0:1] / length
    p5s[1:2, :] = total[1:2] * scale_row / math.sqrt(length)
    p5s[2:4, :] = total[2:4] / math.sqrt(length)

    def last_copy(i, j, mine):
        ch_to = (ch + i) % nch
        own_to = (own + j) % OWN
        here = ch * OWN + own
        there = ch_to * OWN + own_to
        slot = here if mine else there
        return pltpu.make_async_remote_copy(
            src_ref=p5s, dst_ref=p5r.at[slot], send_sem=s5.at[there], recv_sem=r5.at[slot],
            device_id=(sup * OWN + own_to, ch_to), device_id_type=MESH,
        )

    @pl.loop(1, nch * OWN)
    def _(n):
        last_copy(n // OWN, n % OWN, True).start()

    p5r[ch * OWN + own] = p5s[...]

    sent_own(p1s, p1r, s1, r1)
    sent_own(pbs, pbr, sb_, rb_)
    sent_own(p3s, p3r, s3, r3)

    @pl.loop(1, nsb)
    def _(j):
        sup_copy(j, sup).wait_send()
        grad_copy(j, sup).wait_send()

    @pl.loop(1, nch * OWN)
    def _(n):
        last_copy(n // OWN, n % OWN, False).wait_recv()

    @pl.loop(1, nch * OWN)
    def _(n):
        last_copy(n // OWN, n % OWN, True).wait_send()

    g_ref[...] = p5r[...]


def exchange(queries, key_input, value_input, cotangent, residues, log_rates, skip_row):
    nsb = lax.axis_size("ctx") // OWN
    nch = lax.axis_size("ch")
    width = OWN * BLK
    vmem = pl.BlockSpec(memory_space=pltpu.VMEM)
    dma = pltpu.SemaphoreType.DMA
    state = (POLES, BLK)
    return pl.pallas_call(
        functools.partial(comm_kernel, nsb, nch),
        out_shape=(
            jax.ShapeDtypeStruct((TOK, width), BF16),
            jax.ShapeDtypeStruct((TOK, width), BF16),
            jax.ShapeDtypeStruct((nch * OWN, 4, BLK), F32),
        ),
        in_specs=[vmem] * 7,
        out_specs=(vmem, vmem, vmem),
        scratch_shapes=[
            pltpu.VMEM((TOK, width), BF16),
            pltpu.VMEM((TOK, width), BF16),
            *[pltpu.VMEM((OWN, BLK, TOK), BF16)] * 4,
            pltpu.VMEM((OWN, GROUP, TOK), F32),
            pltpu.VMEM((OWN, GROUP, TOK), F32),
            pltpu.VMEM((TOK, width), F32),
            pltpu.VMEM((TOK, width), F32),
            pltpu.VMEM((OWN, 4) + state, BF16),
            pltpu.VMEM((OWN, 4) + state, BF16),
            pltpu.VMEM((2,) + state, BF16),
            pltpu.VMEM((nsb,) + state, BF16),
            pltpu.VMEM((OWN, 2) + state, BF16),
            pltpu.VMEM((OWN, 2) + state, BF16),
            pltpu.VMEM((OWN, 4, BLK), F32),
            pltpu.VMEM((OWN, 4, BLK), F32),
            pltpu.VMEM((4, BLK), F32),
            pltpu.VMEM((nsb, 4, BLK), F32),
            pltpu.VMEM((4, BLK), F32),
            pltpu.VMEM((nch * OWN, 4, BLK), F32),
            dma((OWN,)), dma((OWN,)),
            dma((nsb,)), dma((nsb,)),
            dma((OWN,)), dma((OWN,)),
            dma((OWN,)), dma((OWN,)),
            dma((nsb,)), dma((nsb,)),
            dma((nch * OWN,)), dma((nch * OWN,)),
        ],
        compiler_params=pltpu.CompilerParams(
            collective_id=0, has_side_effects=True, vmem_limit_bytes=48 << 20
        ),
        name="exchange",
    )(queries, key_input, value_input, cotangent, residues, log_rates, skip_row)


def finish_kernel(z_ref, f_ref, c_ref, k_ref, v_ref, g_ref, gq_ref, gk_ref, gv_ref, gr_ref, gl_ref, gs_ref):
    gq_ref[...] = (c_ref[...].astype(F32) * z_ref[...].astype(F32)).astype(BF16)
    flow = f_ref[...].astype(F32)
    gk_ref[...] = (flow * v_ref[...].astype(F32)).astype(BF16)
    gv_ref[...] = (flow * k_ref[...].astype(F32)).astype(BF16)

    @pl.when(pl.program_id(0) == 0)
    def _():
        owners = g_ref.shape[0]
        keep = (iota((owners * 16, BLK), 1) % 16) == (iota((owners * 16, BLK), 0) % 16)
        by_pole = ((iota((BLK, POLES), 0) // 16) == iota((BLK, POLES), 1)).astype(BF16)
        for n, out in ((0, gr_ref), (1, gl_ref)):
            wide = jnp.broadcast_to(g_ref[:, n : n + 1, :], (owners, 16, BLK)).reshape(owners * 16, BLK)
            wide = jnp.where(keep, wide, 0.0)
            hi = wide.astype(BF16)
            mid = (wide - hi.astype(F32)).astype(BF16)
            low = (wide - hi.astype(F32) - mid.astype(F32)).astype(BF16)
            out[...] = dot(hi, by_pole) + dot(mid, by_pole) + dot(low, by_pole)
        gs_ref[...] = g_ref[:, 2, :]


def finish(z, f, cotangent, key_input, value_input, rows):
    width = z.shape[1]
    tile = 512
    owners = rows.shape[0]
    col = pl.BlockSpec((TOK, tile), lambda i: (0, i))

    def whole(shape):
        return pl.BlockSpec(shape, lambda i: (0,) * len(shape))

    return pl.pallas_call(
        finish_kernel,
        grid=(width // tile,),
        out_shape=(
            *[jax.ShapeDtypeStruct((TOK, width), BF16)] * 3,
            jax.ShapeDtypeStruct((owners * 16, POLES), F32),
            jax.ShapeDtypeStruct((owners * 16, POLES), F32),
            jax.ShapeDtypeStruct((owners, BLK), F32),
        ),
        in_specs=[col] * 5 + [whole(rows.shape)],
        out_specs=(col, col, col, whole((owners * 16, POLES)), whole((owners * 16, POLES)), whole((owners, BLK))),
        name="finish",
    )(z, f, cotangent, key_input, value_input, rows)


def local(queries, key_input, value_input, cotangent, residues, log_rates, skip_gain):
    z, f, rows = exchange(
        queries, key_input, value_input, cotangent, residues, log_rates, skip_gain.reshape(1, -1)
    )
    gq, gk, gv, gr, gl, gs = finish(z, f, cotangent, key_input, value_input, rows)
    return (gq, gk, gv, gr, gl, gs.reshape(-1))


def solution(mesh):
    placed = (P("ctx", "ch"), P("ctx", "ch"), P("ctx", "ch"), P("ctx", "ch"), P(), P(), P())
    return jax.shard_map(
        local,
        mesh=mesh,
        in_specs=placed,
        out_specs=(P("ctx", "ch"), P("ctx", "ch"), P("ctx", "ch"), P(), P(), P()),
        check_vma=False,
    )
```

time: 1370 us -> 69.8 us (0.05)
  blocking collectives: 1060 us -> 0 us
  waiting for transfers between devices: 115 us -> 0 us
  Pallas kernels: 0 us -> 58.3 us
  starting transfers between devices: 58 us -> 0 us
  local copies, waits for them, and re-layouts: 59.4 us -> 10.3 us
  matrix products: 39.8 us -> 0 us
  other arithmetic: 22.9 us -> 0 us
    unnamed x1 -> x0, blocking collectives: 799 us -> none
    all_gather x4 -> x0, blocking collectives: 263 us -> none  [the longest x1 229 us: local(): lax.all_gather(grad_log, 'ctx', axis=0, tiled=True)]
    all_to_all x7 -> x0, waiting for transfers between devices: 115 us -> none  [the longest x1 22 us: local(): lax.all_to_all(by_block(cotangent), 'ctx', split_axis=1, concat_axis=0, t...]
    pallas_call x0 -> x2, Pallas kernels: none -> 58.3 us  [the longest x1 53.4 us: exchange(): pl.pallas_call(functools.partial(comm_kernel, nsb, nch), out_shape=(jax.S...]
    all_to_all x7 -> x0, starting transfers between devices: 58 us -> none  [the longest x1 20.8 us: local(): lax.all_to_all(by_block(cotangent), 'ctx', split_axis=1, concat_axis=0, t...]
    slice x10 -> x0, local copies, waits for them, and re-layouts: 40.9 us -> none  [the longest x4 39.2 us: mirror_spectrum(): flipped = jnp.roll(jnp.flip(spectrum, (1, 2)), 1, axis=1)]
    dot_general x24 -> x0, matrix products: 39.8 us -> none  [the longest x12 19.7 us: contract_last(): return jnp.einsum('mkn,nb->mkb', operand, phases, precision=highest)]
  transfers between devices with their start and end apart: 7 -> 0, of which waited for: 6 -> 0; matrix products, arithmetic and copies ran while one was open for 2% -> 0% of each run, Pallas kernels for 0% -> 0%
where the time goes in v1:
time: 69.8 us; the launch traced here: 69.3 us
  Pallas kernels  58.3 us (84%)
  local copies, waits for them, and re-layouts  10.3 us (15%)
  between operations  0.72 us (1%)
    pallas_call x1, Pallas kernels, exchange(): pl.pallas_call(functools.partial(comm_kernel, nsb, nch), out_shape=(jax.S...  53.4 us
    unnamed x25, local copies, waits for them, and re-layouts  10.3 us
    pallas_call x1, Pallas kernels, finish(): pl.pallas_call(finish_kernel, grid=(width // tile,), out_shape=(*[jax.Sha...  4.9 us

profile of v1, /device:TPU:1, one launch (start us, length us, event | category | flops | bytes accessed | tf_op | source)
XLA Modules:
  0.0 69.3 jit_solution(5258870109725175829)
XLA Ops:
  0.6 0.0 copy-start
  0.6 0.9 %copy.13.res_ref = f32[512,16]{1,0:T(8,128)S(1)} copy(f32[512,16]{0,1:T(8,128)} %param.11) | data formatting | bytes 65536 | tf_op args[4]
  1.6 0.0 copy-start.7
  1.6 0.9 %copy.14.log_ref = f32[512,16]{1,0:T(8,128)S(1)} copy(f32[512,16]{0,1:T(8,128)} %param.12) | data formatting | bytes 65536 | tf_op args[5]
  2.5 0.0 copy-done
  2.5 0.0 copy-done.7
  2.5 0.0 copy-start.1
  2.5 1.0 %copy-done.1 = bf16[128,2048]{1,0:T(8,128)(2,1)S(1)} copy-done((bf16[128,2048]{1,0:T(8,128)(2,1)S(1)}, bf16[128,2048]{1,0:T(8,128)(2,1)}, u32[]{:S(2)}) %copy-start.1) | copy-done | bytes 524312
  3.6 0.0 copy-start.2
  3.6 1.0 %copy-done.2 = bf16[128,2048]{1,0:T(8,128)(2,1)S(1)} copy-done((bf16[128,2048]{1,0:T(8,128)(2,1)S(1)}, bf16[128,2048]{1,0:T(8,128)(2,1)}, u32[]{:S(2)}) %copy-start.2) | copy-done | bytes 524312
  4.6 0.0 copy-start.3
  4.6 1.0 %copy-done.3 = bf16[128,2048]{1,0:T(8,128)(2,1)S(1)} copy-done((bf16[128,2048]{1,0:T(8,128)(2,1)S(1)}, bf16[128,2048]{1,0:T(8,128)(2,1)}, u32[]{:S(2)}) %copy-start.3) | copy-done | bytes 524312
  5.6 53.4 %exchange.1 = (bf16[128,2048]{1,0:T(8,128)(2,1)S(1)}, bf16[128,2048]{1,0:T(8,128)(2,1)S(1)}, f32[32,4,256]{2,1,0:T(4,128)S(1)}) custom-call(bf16[128,2048]{1,0:T(8,128)(2,1)S(1)} %copy-done.3, bf16[128,2048]{1,0:T(8,128)(2,1)S(1)} %copy-done, bf16[128,2048]{1,0:T(8,128)(2,1)S(1)} %copy-done.1, bf16[128,2048]{1,0:T(8,128)(2,1)S(1)} %copy-done.2, ...), custom_call_target="tpu_custom_call" | custom-call | tf_op jit(solution)/shard_map/exchange/pallas_call | solution.py:361
  59.0 0.0 copy-start.4
  59.0 0.8 %copy-done.4 = bf16[128,2048]{1,0:T(8,128)(2,1)} copy-done((bf16[128,2048]{1,0:T(8,128)(2,1)}, bf16[128,2048]{1,0:T(8,128)(2,1)S(1)}, u32[]{:S(2)}) %copy-start.4) | copy-done | bytes 524312
  59.8 0.0 copy-start.5
  59.8 0.8 %copy-done.5 = bf16[128,2048]{1,0:T(8,128)(2,1)} copy-done((bf16[128,2048]{1,0:T(8,128)(2,1)}, bf16[128,2048]{1,0:T(8,128)(2,1)S(1)}, u32[]{:S(2)}) %copy-start.5) | copy-done | bytes 524312
  60.6 0.0 copy-start.6
  60.6 0.7 copy-done.6
  61.3 4.9 %finish.1 = (bf16[128,2048]{1,0:T(8,128)(2,1)}, bf16[128,2048]{1,0:T(8,128)(2,1)}, bf16[128,2048]{1,0:T(8,128)(2,1)}, f32[512,16]{1,0:T(8,128)}, f32[512,16]{1,0:T(8,128)}, /*index=5*/f32[32,256]{1,0:T(8,128)}) custom-call(bf16[128,2048]{1,0:T(8,128)(2,1)} %copy-done.4, bf16[128,2048]{1,0:T(8,128)(2,1)} %copy-done.5, bf16[128,2048]{1,0:T(8,128)(2,1)} %c_ref.3, ...), custom_call_target="tpu_custom_call" | custom-call | tf_op jit(solution)/shard_map/finish/pallas_call | solution.py:434
  66.2 0.0 copy-start.8
  66.2 1.7 %copy.15 = f32[512,16]{0,1:T(8,128)} copy(f32[512,16]{1,0:T(8,128)} %get-tuple-element.27) | data formatting | bytes 65536
  67.9 0.0 copy-done.8
  67.9 0.0 copy-start.9
  67.9 0.7 %copy.16 = f32[512,16]{0,1:T(8,128)} copy(f32[512,16]{1,0:T(8,128)S(1)} %copy-done.8) | data formatting | bytes 65536
  68.6 0.0 copy-done.9
  68.7 0.6 copy.17
Async XLA Ops:
  0.6 1.9 %copy-start = (bf16[128,2048]{1,0:T(8,128)(2,1)S(1)}, bf16[128,2048]{1,0:T(8,128)(2,1)}, u32[]{:S(2)}) copy-start(bf16[128,2048]{1,0:T(8,128)(2,1)} %k_ref.3) | copy-start | bytes 1572868
  1.6 0.9 %copy-start.7 = (f32[8192]{0:T(1024)S(1)}, f32[8192]{0:T(1024)}, u32[]{:S(2)}) copy-start(f32[8192]{0:T(1024)} %param.13) | copy-start | bytes 98308
  2.5 1.0 %copy-start.1 = (bf16[128,2048]{1,0:T(8,128)(2,1)S(1)}, bf16[128,2048]{1,0:T(8,128)(2,1)}, u32[]{:S(2)}) copy-start(bf16[128,2048]{1,0:T(8,128)(2,1)} %v_ref.3) | copy-start | bytes 1572868
  3.6 1.0 %copy-start.2 = (bf16[128,2048]{1,0:T(8,128)(2,1)S(1)}, bf16[128,2048]{1,0:T(8,128)(2,1)}, u32[]{:S(2)}) copy-start(bf16[128,2048]{1,0:T(8,128)(2,1)} %c_ref.3) | copy-start | bytes 1572868
  4.6 1.0 %copy-start.3 = (bf16[128,2048]{1,0:T(8,128)(2,1)S(1)}, bf16[128,2048]{1,0:T(8,128)(2,1)}, u32[]{:S(2)}) copy-start(bf16[128,2048]{1,0:T(8,128)(2,1)} %q_ref.1) | copy-start | bytes 1572868
  59.0 0.8 %copy-start.4 = (bf16[128,2048]{1,0:T(8,128)(2,1)}, bf16[128,2048]{1,0:T(8,128)(2,1)S(1)}, u32[]{:S(2)}) copy-start(bf16[128,2048]{1,0:T(8,128)(2,1)S(1)} %get-tuple-element.15.z_ref) | copy-start | bytes 1572868
  59.8 0.8 %copy-start.5 = (bf16[128,2048]{1,0:T(8,128)(2,1)}, bf16[128,2048]{1,0:T(8,128)(2,1)S(1)}, u32[]{:S(2)}) copy-start(bf16[128,2048]{1,0:T(8,128)(2,1)S(1)} %get-tuple-element.16.f_ref) | copy-start | bytes 1572868
  60.6 0.7 copy-start.6
  66.2 1.7 %copy-start.8 = (f32[512,16]{1,0:T(8,128)S(1)}, f32[512,16]{1,0:T(8,128)}, u32[]{:S(2)}) copy-start(f32[512,16]{1,0:T(8,128)} %get-tuple-element.28) | copy-start | bytes 98308
  67.9 0.8 %copy-start.9 = (f32[32,256]{1,0:T(8,128)S(1)}, f32[32,256]{1,0:T(8,128)}, u32[]{:S(2)}) copy-start(f32[32,256]{1,0:T(8,128)} %get-tuple-element.23) | copy-start | bytes 98308

commit v2 on v1

--- a/solution.py
+++ b/solution.py
@@ -32,8 +32,9 @@
 
 def comm_kernel(
     nsb, nch,
-    q_ref, k_ref, v_ref, c_ref, res_ref, log_ref, skip_ref,
-    z_ref, f_ref, g_ref,
+    q_hbm, k_hbm, v_hbm, c_hbm, res_hbm, log_hbm, skip_hbm,
+    gq_ref, gk_ref, gv_ref, gr_ref, gl_ref, gs_ref,
+    q_ref, k_ref, v_ref, c_ref, in_sem, log_ref, res_ref, skip_ref, par_sem, lam_s, res_s,
     x_s, d_s, ed_s, el_s, ed2_s, el2_s, h_s, hr_s, zl_s, fl_s,
     p1s, p1r, p2s, p2r, p3s, p3r, pbs, pbr, p4s, p4r, p5s, p5r,
     s1, r1, s2, r2, s3, r3, sb_, rb_, s4, r4, s5, r5,
@@ -43,6 +44,26 @@
     own = ctx % OWN
     sup = ctx // OWN
 
+    def load(i, n):
+        cols = pl.ds(pl.multiple_of(i * BLK, BLK), BLK)
+        src, dst = ((q_hbm, q_ref), (k_hbm, k_ref), (v_hbm, v_ref), (c_hbm, c_ref))[n]
+        return pltpu.make_async_copy(src.at[:, cols], dst.at[:, cols], in_sem.at[i, n])
+
+    shard = pl.ds(pl.multiple_of(ch * TOK, TOK), TOK)
+    wide_shard = pl.ds(pl.multiple_of(ch * (OWN * BLK), OWN * BLK), OWN * BLK)
+    params = [
+        pltpu.make_async_copy(log_hbm.at[:, shard], log_ref, par_sem.at[0]),
+        pltpu.make_async_copy(res_hbm.at[:, shard], res_ref, par_sem.at[1]),
+        pltpu.make_async_copy(skip_hbm.at[:, wide_shard], skip_ref, par_sem.at[2]),
+    ]
+    for copy in params:
+        copy.start()
+
+    @pl.loop(0, OWN)
+    def _(i):
+        for n in range(4):
+            load(i, n).start()
+
     barrier = pltpu.get_barrier_semaphore()
 
     def greet(ctx_to, ch_to):
@@ -67,12 +88,16 @@
     pick_pole = ((iota((POLES, BLK), 1) // 16) == iota((POLES, BLK), 0)).astype(BF16)
     spread_pole = ((iota((BLK, POLES), 0) // 16) == iota((BLK, POLES), 1)).astype(BF16)
 
-    @pl.loop(0, OWN)
-    def _(i):
-        rows = pl.ds(pl.multiple_of(ch * 128 + i * 16, 16), 16)
-        cols = pl.ds(pl.multiple_of(i * BLK, BLK), BLK)
-        lam = jnp.exp(log_ref[rows, :])
-        res = res_ref[rows, :]
+    for copy in params:
+        copy.wait()
+    lam_s[...] = jnp.exp(log_ref[...]).T
+    res_s[...] = res_ref[...].T
+
+    @pl.loop(0, OWN)
+    def _(i):
+        rows = pl.ds(pl.multiple_of(i * 16, 16), 16)
+        lam = lam_s[rows, :]
+        res = res_s[rows, :]
         taps = jnp.zeros((GROUP, TOK), F32)
         back = jnp.zeros((GROUP, TOK), F32)
         for p in range(POLES):
@@ -89,6 +114,12 @@
             back = back + (res_p * jnp.exp(-lam_p)) * el
         h_s[i] = taps
         hr_s[i] = jnp.where(lane_t == 0.0, taps, back)
+
+    @pl.loop(0, OWN)
+    def _(i):
+        cols = pl.ds(pl.multiple_of(i * BLK, BLK), BLK)
+        for n in range(4):
+            load(i, n).wait()
         x = (k_ref[:, cols].astype(F32) * v_ref[:, cols].astype(F32)).astype(BF16)
         d = (c_ref[:, cols].astype(F32) * q_ref[:, cols].astype(F32)).astype(BF16)
         x_s[:, cols] = x
@@ -151,9 +182,9 @@
             acc = jnp.where(lane_group == g, dot(mat, x), acc)
         zl_s[:, cols] = acc
 
-    rows = pl.ds(pl.multiple_of(ch * 128 + own * 16, 16), 16)
-    lam_own = jnp.exp(log_ref[rows, :])
-    res_own = res_ref[rows, :]
+    rows = pl.ds(pl.multiple_of(own * 16, 16), 16)
+    lam_own = lam_s[rows, :]
+    res_own = res_s[rows, :]
     to_chan = ((iota((16, BLK), 1) // 16) == iota((16, BLK), 0)).astype(F32)
     lam_pc = dot(lam_own, to_chan, ((0,), (0,)), HIGHEST)
     res_pc = dot(res_own, to_chan, ((0,), (0,)), HIGHEST)
@@ -289,14 +320,18 @@
     @pl.loop(0, OWN)
     def _(i):
         cols = pl.ds(pl.multiple_of(i * BLK, BLK), BLK)
-        skip = skip_ref[:, pl.ds(pl.multiple_of(ch * (OWN * BLK) + i * BLK, BLK), BLK)]
-        for n, (table, src, loc, out) in enumerate(
-            ((ed_s, x_s, zl_s, z_ref), (el_s, d_s, fl_s, f_ref))
-        ):
+        skip = skip_ref[:, cols]
+        both = []
+        for n, (table, src, loc) in enumerate(((ed_s, x_s, zl_s), (el_s, d_s, fl_s))):
             wide = dot(spread_pole, p3r[i, n])
             wide = jnp.where(same_group, wide, 0.0).astype(BF16)
             corr = dot(table[i], wide, ((0,), (0,)))
-            out[:, cols] = (skip * src[:, cols].astype(F32) + (loc[:, cols] + corr)).astype(BF16)
+            out = skip * src[:, cols].astype(F32) + (loc[:, cols] + corr)
+            both.append(out.astype(BF16).astype(F32))
+        hidden, flow = both
+        gq_ref[:, cols] = (c_ref[:, cols].astype(F32) * hidden).astype(BF16)
+        gk_ref[:, cols] = (flow * v_ref[:, cols].astype(F32)).astype(BF16)
+        gv_ref[:, cols] = (flow * k_ref[:, cols].astype(F32)).astype(BF16)
 
     to_pole = ((iota((POLES, BLK), 1) // 16) == iota((POLES, BLK), 0)).astype(F32)
     scale = dot(-lam_own * res_own, to_pole, precision=HIGHEST)
@@ -348,7 +383,28 @@
     def _(n):
         last_copy(n // OWN, n % OWN, True).wait_send()
 
-    g_ref[...] = p5r[...]
+    place = (
+        (iota((OWN * BLK, TOK), 0) // BLK == iota((OWN * BLK, TOK), 1) // 16)
+        & (iota((OWN * BLK, TOK), 0) % 16 == iota((OWN * BLK, TOK), 1) % 16)
+    ).astype(BF16)
+    keep = (iota((POLES, OWN * BLK), 1) % BLK) // 16 == iota((POLES, OWN * BLK), 0)
+    for i in range(nch):
+        parts = []
+        for n in range(2):
+            row = jnp.concatenate([p5r[i * OWN + j, n : n + 1, :] for j in range(OWN)], axis=1)
+            hi = row.astype(BF16).astype(F32)
+            mid = (row - hi).astype(BF16).astype(F32)
+            for piece in (hi, mid, row - hi - mid):
+                parts.append(jnp.where(keep, jnp.broadcast_to(piece, keep.shape), 0.0).astype(BF16))
+        got = dot(jnp.concatenate(parts, axis=0), place)
+        for n, out in enumerate((gr_ref, gl_ref)):
+            at = n * 3 * POLES
+            out[:, i * TOK : (i + 1) * TOK] = (
+                got[at : at + POLES] + got[at + POLES : at + 2 * POLES] + got[at + 2 * POLES : at + 3 * POLES]
+            )
+        for j in range(OWN):
+            n = i * OWN + j
+            gs_ref[:, n * BLK : (n + 1) * BLK] = p5r[n, 2:3, :]
 
 
 def exchange(queries, key_input, value_input, cotangent, residues, log_rates, skip_row):
@@ -361,13 +417,21 @@
     return pl.pallas_call(
         functools.partial(comm_kernel, nsb, nch),
         out_shape=(
-            jax.ShapeDtypeStruct((TOK, width), BF16),
-            jax.ShapeDtypeStruct((TOK, width), BF16),
-            jax.ShapeDtypeStruct((nch * OWN, 4, BLK), F32),
+            *[jax.ShapeDtypeStruct((TOK, width), BF16)] * 3,
+            *[jax.ShapeDtypeStruct((POLES, nch * TOK), F32)] * 2,
+            jax.ShapeDtypeStruct((1, nch * width), F32),
         ),
-        in_specs=[vmem] * 7,
-        out_specs=(vmem, vmem, vmem),
+        in_specs=[pl.BlockSpec(memory_space=pltpu.HBM)] * 7,
+        out_specs=(vmem,) * 6,
         scratch_shapes=[
+            *[pltpu.VMEM((TOK, width), BF16)] * 4,
+            dma((OWN, 4)),
+            pltpu.VMEM((POLES, TOK), F32),
+            pltpu.VMEM((POLES, TOK), F32),
+            pltpu.VMEM((1, width), F32),
+            dma((3,)),
+            pltpu.VMEM((TOK, POLES), F32),
+            pltpu.VMEM((TOK, POLES), F32),
             pltpu.VMEM((TOK, width), BF16),
             pltpu.VMEM((TOK, width), BF16),
             *[pltpu.VMEM((OWN, BLK, TOK), BF16)] * 4,
@@ -398,60 +462,42 @@
             collective_id=0, has_side_effects=True, vmem_limit_bytes=48 << 20
         ),
         name="exchange",
-    )(queries, key_input, value_input, cotangent, residues, log_rates, skip_row)
-
-
-def finish_kernel(z_ref, f_ref, c_ref, k_ref, v_ref, g_ref, gq_ref, gk_ref, gv_ref, gr_ref, gl_ref, gs_ref):
-    gq_ref[...] = (c_ref[...].astype(F32) * z_ref[...].astype(F32)).astype(BF16)
-    flow = f_ref[...].astype(F32)
-    gk_ref[...] = (flow * v_ref[...].astype(F32)).astype(BF16)
-    gv_ref[...] = (flow * k_ref[...].astype(F32)).astype(BF16)
-
-    @pl.when(pl.program_id(0) == 0)
-    def _():
-        owners = g_ref.shape[0]
-        keep = (iota((owners * 16, BLK), 1) % 16) == (iota((owners * 16, BLK), 0) % 16)
-        by_pole = ((iota((BLK, POLES), 0) // 16) == iota((BLK, POLES), 1)).astype(BF16)
-        for n, out in ((0, gr_ref), (1, gl_ref)):
-            wide = jnp.broadcast_to(g_ref[:, n : n + 1, :], (owners, 16, BLK)).reshape(owners * 16, BLK)
-            wide = jnp.where(keep, wide, 0.0)
-            hi = wide.astype(BF16)
-            mid = (wide - hi.astype(F32)).astype(BF16)
-            low = (wide - hi.astype(F32) - mid.astype(F32)).astype(BF16)
-            out[...] = dot(hi, by_pole) + dot(mid, by_pole) + dot(low, by_pole)
-        gs_ref[...] = g_ref[:, 2, :]
-
-
-def finish(z, f, cotangent, key_input, value_input, rows):
-    width = z.shape[1]
-    tile = 512
-    owners = rows.shape[0]
-    col = pl.BlockSpec((TOK, tile), lambda i: (0, i))
-
-    def whole(shape):
-        return pl.BlockSpec(shape, lambda i: (0,) * len(shape))
-
+    )(
+        *[
+            pltpu.with_memory_space_constraint(val, pltpu.HBM)
+            for val in (queries, key_input, value_input, cotangent, residues, log_rates, skip_row)
+        ]
+    )
+
+
+def store_kernel(*refs):
+    count = (len(refs) - 1) // 2
+    sem = refs[-1]
+    copies = [pltpu.make_async_copy(refs[n], refs[count + n], sem.at[n]) for n in range(count)]
+    for copy in copies:
+        copy.start()
+    for copy in copies:
+        copy.wait()
+
+
+def store(*arrays):
+    count = len(arrays)
     return pl.pallas_call(
-        finish_kernel,
-        grid=(width // tile,),
-        out_shape=(
-            *[jax.ShapeDtypeStruct((TOK, width), BF16)] * 3,
-            jax.ShapeDtypeStruct((owners * 16, POLES), F32),
-            jax.ShapeDtypeStruct((owners * 16, POLES), F32),
-            jax.ShapeDtypeStruct((owners, BLK), F32),
-        ),
-        in_specs=[col] * 5 + [whole(rows.shape)],
-        out_specs=(col, col, col, whole((owners * 16, POLES)), whole((owners * 16, POLES)), whole((owners, BLK))),
-        name="finish",
-    )(z, f, cotangent, key_input, value_input, rows)
+        store_kernel,
+        out_shape=tuple(jax.ShapeDtypeStruct(val.shape, val.dtype) for val in arrays),
+        in_specs=[pl.BlockSpec(memory_space=pltpu.VMEM)] * count,
+        out_specs=(pl.BlockSpec(memory_space=pltpu.HBM),) * count,
+        scratch_shapes=[pltpu.SemaphoreType.DMA((count,))],
+        compiler_params=pltpu.CompilerParams(vmem_limit_bytes=1 << 20),
+        name="store",
+    )(*arrays)
 
 
 def local(queries, key_input, value_input, cotangent, residues, log_rates, skip_gain):
-    z, f, rows = exchange(
-        queries, key_input, value_input, cotangent, residues, log_rates, skip_gain.reshape(1, -1)
-    )
-    gq, gk, gv, gr, gl, gs = finish(z, f, cotangent, key_input, value_input, rows)
-    return (gq, gk, gv, gr, gl, gs.reshape(-1))
+    gq, gk, gv, gr, gl, gs = store(*exchange(
+        queries, key_input, value_input, cotangent, residues.T, log_rates.T, skip_gain.reshape(1, -1)
+    ))
+    return (gq, gk, gv, gr.T, gl.T, gs.reshape(-1))
 
 
 def solution(mesh):

time: 69.8 us -> 57.5 us (0.82)
  local copies, waits for them, and re-layouts: 10.3 us -> 0 us
  Pallas kernels: 58.3 us -> 56.7 us
    unnamed x25 -> x0, local copies, waits for them, and re-layouts: 10.3 us -> none
    pallas_call x2, Pallas kernels: 58.3 us -> 56.7 us  [the longest x1 55.5 us: exchange(): pl.pallas_call(functools.partial(comm_kernel, nsb, nch), out_shape=(*[jax...]
where the time goes in v2:
time: 57.5 us; the launch traced here: 57.4 us
  Pallas kernels  56.7 us (99%)
  between operations  0.64 us (1%)
    pallas_call x1, Pallas kernels, exchange(): pl.pallas_call(functools.partial(comm_kernel, nsb, nch), out_shape=(*[jax...  55.5 us
    pallas_call x1, Pallas kernels, store(): pl.pallas_call(store_kernel, out_shape=tuple((jax.ShapeDtypeStruct(val.sh...  1.21 us

profile of v2, /device:TPU:1, one launch (start us, length us, event | category | flops | bytes accessed | tf_op | source)
XLA Modules:
  0.0 57.4 jit_solution(6169903398522522233)
XLA Ops:
  0.6 55.5 %exchange.1 = (bf16[128,2048]{1,0:T(8,128)(2,1)S(1)}, bf16[128,2048]{1,0:T(8,128)(2,1)S(1)}, bf16[128,2048]{1,0:T(8,128)(2,1)S(1)}, f32[16,512]{1,0:T(8,128)S(1)...) custom-call(bf16[128,2048]{1,0:T(8,128)(2,1)} %q_hbm.1, bf16[128,2048]{1,0:T(8,128)(2,1)} %k_hbm.1, ...), custom_call_target="tpu_custom_call" | custom-call | tf_op jit(solution)/shard_map/exchange/pallas_call | solution.py:417
  56.2 1.2 %store.1 = (bf16[128,2048]{1,0:T(8,128)(2,1)}, bf16[128,2048]{1,0:T(8,128)(2,1)}, bf16[128,2048]{1,0:T(8,128)(2,1)}, f32[16,512]{1,0:T(8,128)}, f32[16,512]{1,0:T(8,128)}, /*index=5*/f32[1,8192]{1,0:T(1,128)}) custom-call(bf16[128,2048]{1,0:T(8,128)(2,1)S(1)} %get-tuple-element.18.refs_0_, bf16[128,2048]{1,0:T(8,128)(2,1)S(1)} %get-tuple-element.19.refs_1_, ...), custom_call_target="tpu_custom_call" | custom-call | tf_op jit(solution)/shard_map/store/pallas_call | solution.py:485

commit v3 on v2

--- a/solution.py
+++ b/solution.py
@@ -36,8 +36,8 @@
     gq_ref, gk_ref, gv_ref, gr_ref, gl_ref, gs_ref,
     q_ref, k_ref, v_ref, c_ref, in_sem, log_ref, res_ref, skip_ref, par_sem, lam_s, res_s,
     x_s, d_s, ed_s, el_s, ed2_s, el2_s, h_s, hr_s, zl_s, fl_s,
-    p1s, p1r, p2s, p2r, p3s, p3r, pbs, pbr, p4s, p4r, p5s, p5r,
-    s1, r1, s2, r2, s3, r3, sb_, rb_, s4, r4, s5, r5,
+    p1s, p1r, pms, pmr, p2s, p2r, p3s, p3r, pbs, pbr, p4s, p4r, p5s, p5r, coef_s, place_s, swap_s, swap_r, sh,
+    s1, r1, sm, rm, s2, r2, s3, r3, sb_, rb_, s4, r4, s5, r5,
 ):
     ctx = lax.axis_index("ctx")
     ch = lax.axis_index("ch")
@@ -128,7 +128,11 @@
         for n, (table, val) in enumerate(((el_s, x), (ed_s, d), (el2_s, x), (ed2_s, d))):
             full = dot(table[i], val)
             full = jnp.where(same_group, full, 0.0).astype(BF16)
-            p1s[i, n] = dot(pick_pole, full).astype(BF16)
+            kept = dot(pick_pole, full).astype(BF16)
+            if n < 2:
+                p1s[i, n] = kept
+            else:
+                pms[i, n - 2] = kept
 
     pl.semaphore_wait(barrier, (OWN - 1) + (nsb - 1) + (nch - 1) * OWN)
 
@@ -162,56 +166,13 @@
             from_own(j, *args).wait_send()
 
     send_own(p1s, p1r, s1, r1)
+    send_own(pms, pmr, sm, rm)
     p1r[own] = p1s[own]
-    p2r[sup] = jnp.zeros((POLES, BLK), BF16)
+    pmr[own] = pms[own]
 
     row_t = iota((TOK, TOK), 0)
     col_t = iota((TOK, TOK), 1)
     lane_group = iota((TOK, BLK), 1) // 16
-
-    @pl.loop(0, OWN)
-    def _(i):
-        cols = pl.ds(pl.multiple_of(i * BLK, BLK), BLK)
-        x = x_s[:, cols]
-        acc = jnp.zeros((TOK, BLK), F32)
-        hr = hr_s[i]
-        for g in range(16):
-            wide = jnp.broadcast_to(hr[g : g + 1, :], (TOK, TOK))
-            mat = pltpu.roll(wide, 0, 1, stride=1, stride_axis=0)
-            mat = jnp.where(col_t <= row_t, mat, 0.0).astype(BF16)
-            acc = jnp.where(lane_group == g, dot(mat, x), acc)
-        zl_s[:, cols] = acc
-
-    rows = pl.ds(pl.multiple_of(own * 16, 16), 16)
-    lam_own = lam_s[rows, :]
-    res_own = res_s[rows, :]
-    to_chan = ((iota((16, BLK), 1) // 16) == iota((16, BLK), 0)).astype(F32)
-    lam_pc = dot(lam_own, to_chan, ((0,), (0,)), HIGHEST)
-    res_pc = dot(res_own, to_chan, ((0,), (0,)), HIGHEST)
-    w = jnp.exp(-float(TOK) * lam_pc)
-    e1 = jnp.exp(-lam_pc)
-    re1 = res_pc * e1
-
-    wait_own(p1s, p1r, s1, r1)
-    sum_l = jnp.zeros((POLES, BLK), F32)
-    sum_d = jnp.zeros((POLES, BLK), F32)
-    for b in range(OWN):
-        sum_l = w * sum_l + p1r[b, 0].astype(F32)
-        sum_d = w * sum_d + p1r[OWN - 1 - b, 1].astype(F32)
-    p2s[0] = sum_l.astype(BF16)
-    p2s[1] = sum_d.astype(BF16)
-
-    def sup_copy(j, slot):
-        other = (sup + j) % nsb
-        later = (other > sup).astype(jnp.int32)
-        return pltpu.make_async_remote_copy(
-            src_ref=p2s.at[1 - later], dst_ref=p2r.at[slot], send_sem=s2.at[other], recv_sem=r2.at[slot],
-            device_id=(other * OWN + own, ch), device_id_type=MESH,
-        )
-
-    @pl.loop(1, nsb)
-    def _(j):
-        sup_copy(j, sup).start()
 
     lane_row = iota((16, BLK), 1)
     diag = (lane_row % 16) == iota((16, BLK), 0)
@@ -244,6 +205,91 @@
     send_own(pbs, pbr, sb_, rb_)
     pbr[own] = pbs[own]
 
+    rows = pl.ds(pl.multiple_of(own * 16, 16), 16)
+    lam_own = lam_s[rows, :]
+    res_own = res_s[rows, :]
+    to_chan = ((iota((16, BLK), 1) // 16) == iota((16, BLK), 0)).astype(F32)
+    lam_pc = dot(lam_own, to_chan, ((0,), (0,)), HIGHEST)
+    res_pc = dot(res_own, to_chan, ((0,), (0,)), HIGHEST)
+    w = jnp.exp(-float(TOK) * lam_pc)
+    e1 = jnp.exp(-lam_pc)
+    re1 = res_pc * e1
+
+    wait_own(p1s, p1r, s1, r1)
+    sum_l = jnp.zeros((POLES, BLK), F32)
+    sum_d = jnp.zeros((POLES, BLK), F32)
+    for b in range(OWN):
+        sum_l = w * sum_l + p1r[b, 0].astype(F32)
+        sum_d = w * sum_d + p1r[OWN - 1 - b, 1].astype(F32)
+    p2s[0] = sum_l.astype(BF16)
+    p2s[1] = sum_d.astype(BF16)
+
+    col = sup // 2
+    half = sup % 2
+    ncol = nsb // 2
+
+    def col_copy(j, slot):
+        other = (col + j) % ncol
+        later = (other > col).astype(jnp.int32)
+        return pltpu.make_async_remote_copy(
+            src_ref=p2s.at[1 - later], dst_ref=p2r.at[slot], send_sem=s2.at[other], recv_sem=r2.at[slot],
+            device_id=((other * 2 + half) * OWN + own, ch), device_id_type=MESH,
+        )
+
+    def half_copy():
+        return pltpu.make_async_remote_copy(
+            src_ref=swap_s, dst_ref=swap_r, send_sem=sh.at[0], recv_sem=sh.at[1],
+            device_id=((col * 2 + 1 - half) * OWN + own, ch), device_id_type=MESH,
+        )
+
+    @pl.loop(1, ncol)
+    def _(j):
+        col_copy(j, col).start()
+
+    scale = dot(
+        -lam_own * res_own, ((iota((POLES, BLK), 1) // 16) == iota((POLES, BLK), 0)).astype(F32), precision=HIGHEST
+    )
+    scale_row = jnp.sum(jnp.where(diag, scale, 0.0), axis=0, keepdims=True)
+
+    @pl.loop(0, ncol)
+    def _(b):
+        gap = jnp.maximum(jnp.abs(col - b) - 1, 0).astype(F32) * float(TOK * OWN * 2)
+        coef_s[b] = jnp.exp(-lam_pc * gap)
+
+    wide_w = jnp.exp(-float(TOK * OWN) * lam_pc)
+    wide_w2 = jnp.exp(-float(TOK * OWN * 2) * lam_pc)
+
+    place_s[...] = (
+        (iota((OWN * BLK, TOK), 0) // BLK == iota((OWN * BLK, TOK), 1) // 16)
+        & (iota((OWN * BLK, TOK), 0) % 16 == iota((OWN * BLK, TOK), 1) % 16)
+    ).astype(BF16)
+    @pl.loop(0, OWN)
+    def _(i):
+        cols = pl.ds(pl.multiple_of(i * BLK, BLK), BLK)
+        x = x_s[:, cols]
+        acc = jnp.zeros((TOK, BLK), F32)
+        hr = hr_s[i]
+        for g in range(16):
+            wide = jnp.broadcast_to(hr[g : g + 1, :], (TOK, TOK))
+            mat = pltpu.roll(wide, 0, 1, stride=1, stride_axis=0)
+            mat = jnp.where(col_t <= row_t, mat, 0.0).astype(BF16)
+            acc = jnp.where(lane_group == g, dot(mat, x), acc)
+        zl_s[:, cols] = acc
+
+    zero = jnp.zeros((POLES, BLK), F32)
+
+    def gather(j, sums):
+        other = (col + j) % ncol
+        col_copy(j, other).wait_recv()
+        term = coef_s[other] * p2r[other].astype(F32)
+        later = other > col
+        return sums[0] + jnp.where(later, 0.0, term), sums[1] + jnp.where(later, term, 0.0)
+
+    col_s, col_f = lax.fori_loop(1, ncol, gather, (zero, zero))
+    swap_s[0] = jnp.where(half == 0, sum_l + wide_w2 * col_s, col_s).astype(BF16)
+    swap_s[1] = jnp.where(half == 0, col_f, sum_d + wide_w2 * col_f).astype(BF16)
+    half_copy().start()
+
     @pl.loop(0, OWN)
     def _(i):
         cols = pl.ds(pl.multiple_of(i * BLK, BLK), BLK)
@@ -257,17 +303,15 @@
             acc = jnp.where(lane_group == g, dot(mat, d), acc)
         fl_s[:, cols] = acc
 
-    @pl.loop(1, nsb)
-    def _(j):
-        sup_copy(j, (sup + j) % nsb).wait_recv()
-
-    in_s = jnp.zeros((POLES, BLK), F32)
-    in_f = jnp.zeros((POLES, BLK), F32)
-    for b in range(nsb):
-        gap = jnp.maximum(jnp.abs(sup - b) - 1, 0).astype(F32) * float(TOK * OWN)
-        term = jnp.exp(-lam_pc * gap) * p2r[b].astype(F32)
-        in_s = in_s + jnp.where(b < sup, term, 0.0)
-        in_f = in_f + jnp.where(b > sup, term, 0.0)
+    wait_own(pms, pmr, sm, rm)
+    wait_own(pbs, pbr, sb_, rb_)
+    part = pbr[0]
+    for b in range(1, OWN):
+        part = part + pbr[b]
+
+    half_copy().wait_recv()
+    in_s = wide_w * col_s + swap_r[0].astype(F32)
+    in_f = wide_w * col_f + swap_r[1].astype(F32)
     carry_s = []
     for b in range(OWN):
         carry_s.append(in_s)
@@ -281,26 +325,28 @@
         r_sum = r_sum + d_b * carry_s[b]
         m_sum = (
             m_sum
-            + p1r[b, 3].astype(F32) * carry_s[b]
-            + p1r[b, 2].astype(F32) * in_f
+            + pmr[b, 1].astype(F32) * carry_s[b]
+            + pmr[b, 0].astype(F32) * in_f
             + (float(TOK) * w) * (carry_s[b] * in_f)
         )
         in_f = w * in_f + d_b
-    send_own(p3s, p3r, s3, r3)
-    p3r[own] = p3s[own]
+    def pack(first, second, third):
+        half = BLK // 2
+        top = jnp.concatenate([first, second[:, :half]], axis=1)
+        low = jnp.concatenate([second[:, half:], third], axis=1)
+        return jnp.concatenate([top, low], axis=0).astype(BF16)
+
+    def unpack(val):
+        half = BLK // 2
+        second = jnp.concatenate([val[0:1, BLK:], val[1:2, :half]], axis=1)
+        return val[0:1, :BLK], second, val[1:2, half:]
 
     chan_group = ((iota((BLK, BLK), 0) // 16) == (iota((BLK, BLK), 1) % 16)).astype(F32)
     pole_row = (iota((POLES, BLK), 1) // 16) == iota((POLES, BLK), 0)
     sums = dot(jnp.concatenate([r_sum * e1, m_sum * e1], axis=0), chan_group, precision=HIGHEST)
     r_row = jnp.sum(jnp.where(pole_row, sums[:POLES], 0.0), axis=0, keepdims=True)
     m_row = jnp.sum(jnp.where(pole_row, sums[POLES:], 0.0), axis=0, keepdims=True)
-    wait_own(pbs, pbr, sb_, rb_)
-    part = pbr[0]
-    for b in range(1, OWN):
-        part = part + pbr[b]
-    p4s[0:1, :] = part[0:1] + r_row
-    p4s[1:2, :] = part[1:2] + m_row
-    p4s[2:4, :] = part[2:4]
+    p4s[...] = pack(part[0:1] + r_row, part[1:2] + m_row, part[2:3])
 
     def grad_copy(j, slot):
         other = (sup + j) % nsb
@@ -313,12 +359,18 @@
     def _(j):
         grad_copy(j, sup).start()
 
+    send_own(p3s, p3r, s3, r3)
+    p3r[own] = p3s[own]
     p4r[sup] = p4s[...]
 
-    wait_own(p3s, p3r, s3, r3)
-
-    @pl.loop(0, OWN)
-    def _(i):
+    @pl.loop(0, OWN)
+    def _(j):
+        i = (own + j) % OWN
+
+        @pl.when(j > 0)
+        def _():
+            from_own(j, p3s, p3r, s3, r3).wait_recv()
+
         cols = pl.ds(pl.multiple_of(i * BLK, BLK), BLK)
         skip = skip_ref[:, cols]
         both = []
@@ -333,21 +385,17 @@
         gk_ref[:, cols] = (flow * v_ref[:, cols].astype(F32)).astype(BF16)
         gv_ref[:, cols] = (flow * k_ref[:, cols].astype(F32)).astype(BF16)
 
-    to_pole = ((iota((POLES, BLK), 1) // 16) == iota((POLES, BLK), 0)).astype(F32)
-    scale = dot(-lam_own * res_own, to_pole, precision=HIGHEST)
-    scale_row = jnp.sum(jnp.where(diag, scale, 0.0), axis=0, keepdims=True)
     length = float(TOK * OWN * nsb)
 
     @pl.loop(1, nsb)
     def _(j):
         grad_copy(j, (sup + j) % nsb).wait_recv()
 
-    total = p4r[0]
+    total = p4r[0].astype(F32)
     for b in range(1, nsb):
-        total = total + p4r[b]
-    p5s[0:1, :] = total[0:1] / length
-    p5s[1:2, :] = total[1:2] * scale_row / math.sqrt(length)
-    p5s[2:4, :] = total[2:4] / math.sqrt(length)
+        total = total + p4r[b].astype(F32)
+    r_row, m_row, k_row = unpack(total)
+    p5s[...] = pack(r_row / length, m_row * scale_row / math.sqrt(length), k_row / math.sqrt(length))
 
     def last_copy(i, j, mine):
         ch_to = (ch + i) % nch
@@ -367,12 +415,18 @@
     p5r[ch * OWN + own] = p5s[...]
 
     sent_own(p1s, p1r, s1, r1)
+    sent_own(pms, pmr, sm, rm)
     sent_own(pbs, pbr, sb_, rb_)
     sent_own(p3s, p3r, s3, r3)
 
+    half_copy().wait_send()
+
+    @pl.loop(1, ncol)
+    def _(j):
+        col_copy(j, col).wait_send()
+
     @pl.loop(1, nsb)
     def _(j):
-        sup_copy(j, sup).wait_send()
         grad_copy(j, sup).wait_send()
 
     @pl.loop(1, nch * OWN)
@@ -383,28 +437,19 @@
     def _(n):
         last_copy(n // OWN, n % OWN, True).wait_send()
 
-    place = (
-        (iota((OWN * BLK, TOK), 0) // BLK == iota((OWN * BLK, TOK), 1) // 16)
-        & (iota((OWN * BLK, TOK), 0) % 16 == iota((OWN * BLK, TOK), 1) % 16)
-    ).astype(BF16)
     keep = (iota((POLES, OWN * BLK), 1) % BLK) // 16 == iota((POLES, OWN * BLK), 0)
     for i in range(nch):
+        rows = [unpack(p5r[i * OWN + j].astype(F32)) for j in range(OWN)]
         parts = []
         for n in range(2):
-            row = jnp.concatenate([p5r[i * OWN + j, n : n + 1, :] for j in range(OWN)], axis=1)
-            hi = row.astype(BF16).astype(F32)
-            mid = (row - hi).astype(BF16).astype(F32)
-            for piece in (hi, mid, row - hi - mid):
-                parts.append(jnp.where(keep, jnp.broadcast_to(piece, keep.shape), 0.0).astype(BF16))
-        got = dot(jnp.concatenate(parts, axis=0), place)
-        for n, out in enumerate((gr_ref, gl_ref)):
-            at = n * 3 * POLES
-            out[:, i * TOK : (i + 1) * TOK] = (
-                got[at : at + POLES] + got[at + POLES : at + 2 * POLES] + got[at + 2 * POLES : at + 3 * POLES]
-            )
+            row = jnp.concatenate([val[n] for val in rows], axis=1)
+            parts.append(jnp.where(keep, jnp.broadcast_to(row, keep.shape), 0.0).astype(BF16))
+        got = dot(jnp.concatenate(parts, axis=0), place_s[...])
+        gr_ref[:, i * TOK : (i + 1) * TOK] = got[:POLES]
+        gl_ref[:, i * TOK : (i + 1) * TOK] = got[POLES:]
         for j in range(OWN):
             n = i * OWN + j
-            gs_ref[:, n * BLK : (n + 1) * BLK] = p5r[n, 2:3, :]
+            gs_ref[:, n * BLK : (n + 1) * BLK] = rows[j][2]
 
 
 def exchange(queries, key_input, value_input, cotangent, residues, log_rates, skip_row):
@@ -439,20 +484,25 @@
             pltpu.VMEM((OWN, GROUP, TOK), F32),
             pltpu.VMEM((TOK, width), F32),
             pltpu.VMEM((TOK, width), F32),
-            pltpu.VMEM((OWN, 4) + state, BF16),
-            pltpu.VMEM((OWN, 4) + state, BF16),
+            *[pltpu.VMEM((OWN, 2) + state, BF16)] * 4,
             pltpu.VMEM((2,) + state, BF16),
-            pltpu.VMEM((nsb,) + state, BF16),
+            pltpu.VMEM((nsb // 2,) + state, BF16),
             pltpu.VMEM((OWN, 2) + state, BF16),
             pltpu.VMEM((OWN, 2) + state, BF16),
             pltpu.VMEM((OWN, 4, BLK), F32),
             pltpu.VMEM((OWN, 4, BLK), F32),
-            pltpu.VMEM((4, BLK), F32),
-            pltpu.VMEM((nsb, 4, BLK), F32),
-            pltpu.VMEM((4, BLK), F32),
-            pltpu.VMEM((nch * OWN, 4, BLK), F32),
+            pltpu.VMEM((2, 3 * BLK // 2), BF16),
+            pltpu.VMEM((nsb, 2, 3 * BLK // 2), BF16),
+            pltpu.VMEM((2, 3 * BLK // 2), BF16),
+            pltpu.VMEM((nch * OWN, 2, 3 * BLK // 2), BF16),
+            pltpu.VMEM((nsb // 2,) + state, F32),
+            pltpu.VMEM((OWN * BLK, TOK), BF16),
+            pltpu.VMEM((2,) + state, BF16),
+            pltpu.VMEM((2,) + state, BF16),
+            dma((2,)),
             dma((OWN,)), dma((OWN,)),
-            dma((nsb,)), dma((nsb,)),
+            dma((OWN,)), dma((OWN,)),
+            dma((nsb // 2,)), dma((nsb // 2,)),
             dma((OWN,)), dma((OWN,)),
             dma((OWN,)), dma((OWN,)),
             dma((nsb,)), dma((nsb,)),

time: 57.5 us -> 57.4 us (level)
  no operation moved by 1% of the time
where the time goes in v3:
time: 57.4 us; the launch traced here: 57.3 us
  Pallas kernels  56.6 us (99%)
  between operations  0.64 us (1%)
    pallas_call x1, Pallas kernels, exchange(): pl.pallas_call(functools.partial(comm_kernel, nsb, nch), out_shape=(*[jax...  55.4 us
    pallas_call x1, Pallas kernels, store(): pl.pallas_call(store_kernel, out_shape=tuple((jax.ShapeDtypeStruct(val.sh...  1.21 us

profile of v3, /device:TPU:1, one launch (start us, length us, event | category | flops | bytes accessed | tf_op | source)
XLA Modules:
  0.0 57.3 jit_solution(8005351976849449875)
XLA Ops:
  0.6 55.4 %exchange.1 = (bf16[128,2048]{1,0:T(8,128)(2,1)S(1)}, bf16[128,2048]{1,0:T(8,128)(2,1)S(1)}, bf16[128,2048]{1,0:T(8,128)(2,1)S(1)}, f32[16,512]{1,0:T(8,128)S(1)...) custom-call(bf16[128,2048]{1,0:T(8,128)(2,1)} %q_hbm.1, bf16[128,2048]{1,0:T(8,128)(2,1)} %k_hbm.1, ...), custom_call_target="tpu_custom_call" | custom-call | tf_op jit(solution)/shard_map/exchange/pallas_call | solution.py:462
  56.1 1.2 %store.1 = (bf16[128,2048]{1,0:T(8,128)(2,1)}, bf16[128,2048]{1,0:T(8,128)(2,1)}, bf16[128,2048]{1,0:T(8,128)(2,1)}, f32[16,512]{1,0:T(8,128)}, f32[16,512]{1,0:T(8,128)}, /*index=5*/f32[1,8192]{1,0:T(1,128)}) custom-call(bf16[128,2048]{1,0:T(8,128)(2,1)S(1)} %get-tuple-element.18.refs_0_, bf16[128,2048]{1,0:T(8,128)(2,1)S(1)} %get-tuple-element.19.refs_1_, ...), custom_call_target="tpu_custom_call" | custom-call | tf_op jit(solution)/shard_map/store/pallas_call | solution.py:535

commit v4 on v3

--- a/solution.py
+++ b/solution.py
@@ -97,6 +97,64 @@
     def _(i):
         rows = pl.ds(pl.multiple_of(i * 16, 16), 16)
         lam = lam_s[rows, :]
+        for p in range(POLES):
+            lam_p = lam[:, p : p + 1]
+            at = pl.ds(p * 16, 16)
+            ed_s[i, at, :] = jnp.exp(-lam_p * lane_t).astype(BF16)
+            el_s[i, at, :] = jnp.exp(-lam_p * (TOK - 1.0 - lane_t)).astype(BF16)
+
+    @pl.loop(0, OWN)
+    def _(i):
+        cols = pl.ds(pl.multiple_of(i * BLK, BLK), BLK)
+        for n in range(4):
+            load(i, n).wait()
+        x = (k_ref[:, cols].astype(F32) * v_ref[:, cols].astype(F32)).astype(BF16)
+        d = (c_ref[:, cols].astype(F32) * q_ref[:, cols].astype(F32)).astype(BF16)
+        x_s[:, cols] = x
+        d_s[:, cols] = d
+        for n, (table, val) in enumerate(((el_s, x), (ed_s, d))):
+            full = jnp.where(same_group, dot(table[i], val), 0.0).astype(BF16)
+            p1s[i, n] = dot(pick_pole, full).astype(BF16)
+
+    pl.semaphore_wait(barrier, (OWN - 1) + (nsb - 1) + (nch - 1) * OWN)
+
+    def to_own(j, src, dst, send, recv):
+        other = (own + j) % OWN
+        return pltpu.make_async_remote_copy(
+            src_ref=src.at[other], dst_ref=dst.at[own], send_sem=send.at[other], recv_sem=recv.at[own],
+            device_id=(sup * OWN + other, ch), device_id_type=MESH,
+        )
+
+    def from_own(j, src, dst, send, recv):
+        other = (own + j) % OWN
+        return pltpu.make_async_remote_copy(
+            src_ref=src.at[other], dst_ref=dst.at[other], send_sem=send.at[other], recv_sem=recv.at[other],
+            device_id=(sup * OWN + other, ch), device_id_type=MESH,
+        )
+
+    def send_own(*args):
+        @pl.loop(1, OWN)
+        def _(j):
+            to_own(j, *args).start()
+
+    def wait_own(*args):
+        @pl.loop(1, OWN)
+        def _(j):
+            from_own(j, *args).wait_recv()
+
+    def sent_own(*args):
+        @pl.loop(1, OWN)
+        def _(j):
+            from_own(j, *args).wait_send()
+
+    send_own(p1s, p1r, s1, r1)
+    p1r[own] = p1s[own]
+
+    @pl.loop(0, OWN)
+    def _(i):
+        rows = pl.ds(pl.multiple_of(i * 16, 16), 16)
+        cols = pl.ds(pl.multiple_of(i * BLK, BLK), BLK)
+        lam = lam_s[rows, :]
         res = res_s[rows, :]
         taps = jnp.zeros((GROUP, TOK), F32)
         back = jnp.zeros((GROUP, TOK), F32)
@@ -106,68 +164,20 @@
             ed = jnp.exp(-lam_p * lane_t)
             el = jnp.exp(-lam_p * (TOK - 1.0 - lane_t))
             at = pl.ds(p * 16, 16)
-            ed_s[i, at, :] = ed.astype(BF16)
-            el_s[i, at, :] = el.astype(BF16)
             ed2_s[i, at, :] = (ed * (lane_t + 1.0)).astype(BF16)
             el2_s[i, at, :] = (el * (TOK - 1.0 - lane_t)).astype(BF16)
             taps = taps + res_p * ed
             back = back + (res_p * jnp.exp(-lam_p)) * el
         h_s[i] = taps
         hr_s[i] = jnp.where(lane_t == 0.0, taps, back)
-
-    @pl.loop(0, OWN)
-    def _(i):
-        cols = pl.ds(pl.multiple_of(i * BLK, BLK), BLK)
-        for n in range(4):
-            load(i, n).wait()
-        x = (k_ref[:, cols].astype(F32) * v_ref[:, cols].astype(F32)).astype(BF16)
-        d = (c_ref[:, cols].astype(F32) * q_ref[:, cols].astype(F32)).astype(BF16)
-        x_s[:, cols] = x
-        d_s[:, cols] = d
+        x = x_s[:, cols]
+        d = d_s[:, cols]
         pbs[i, 2:3, :] = jnp.sum(x.astype(F32) * d.astype(F32), axis=0, keepdims=True)
-        for n, (table, val) in enumerate(((el_s, x), (ed_s, d), (el2_s, x), (ed2_s, d))):
-            full = dot(table[i], val)
-            full = jnp.where(same_group, full, 0.0).astype(BF16)
-            kept = dot(pick_pole, full).astype(BF16)
-            if n < 2:
-                p1s[i, n] = kept
-            else:
-                pms[i, n - 2] = kept
-
-    pl.semaphore_wait(barrier, (OWN - 1) + (nsb - 1) + (nch - 1) * OWN)
-
-    def to_own(j, src, dst, send, recv):
-        other = (own + j) % OWN
-        return pltpu.make_async_remote_copy(
-            src_ref=src.at[other], dst_ref=dst.at[own], send_sem=send.at[other], recv_sem=recv.at[own],
-            device_id=(sup * OWN + other, ch), device_id_type=MESH,
-        )
-
-    def from_own(j, src, dst, send, recv):
-        other = (own + j) % OWN
-        return pltpu.make_async_remote_copy(
-            src_ref=src.at[other], dst_ref=dst.at[other], send_sem=send.at[other], recv_sem=recv.at[other],
-            device_id=(sup * OWN + other, ch), device_id_type=MESH,
-        )
-
-    def send_own(*args):
-        @pl.loop(1, OWN)
-        def _(j):
-            to_own(j, *args).start()
-
-    def wait_own(*args):
-        @pl.loop(1, OWN)
-        def _(j):
-            from_own(j, *args).wait_recv()
-
-    def sent_own(*args):
-        @pl.loop(1, OWN)
-        def _(j):
-            from_own(j, *args).wait_send()
-
-    send_own(p1s, p1r, s1, r1)
+        for n, (table, val) in enumerate(((el2_s, x), (ed2_s, d))):
+            full = jnp.where(same_group, dot(table[i], val), 0.0).astype(BF16)
+            pms[i, n] = dot(pick_pole, full).astype(BF16)
+
     send_own(pms, pmr, sm, rm)
-    p1r[own] = p1s[own]
     pmr[own] = pms[own]
 
     row_t = iota((TOK, TOK), 0)
@@ -177,6 +187,78 @@
     lane_row = iota((16, BLK), 1)
     diag = (lane_row % 16) == iota((16, BLK), 0)
     flip = (row_t == TOK - 1 - col_t).astype(BF16)
+
+    rows = pl.ds(pl.multiple_of(own * 16, 16), 16)
+    lam_own = lam_s[rows, :]
+    res_own = res_s[rows, :]
+    to_chan = ((iota((16, BLK), 1) // 16) == iota((16, BLK), 0)).astype(F32)
+    lam_pc = dot(lam_own, to_chan, ((0,), (0,)), HIGHEST)
+    res_pc = dot(res_own, to_chan, ((0,), (0,)), HIGHEST)
+    w = jnp.exp(-float(TOK) * lam_pc)
+    e1 = jnp.exp(-lam_pc)
+    re1 = res_pc * e1
+
+    wait_own(p1s, p1r, s1, r1)
+    sum_l = jnp.zeros((POLES, BLK), F32)
+    sum_d = jnp.zeros((POLES, BLK), F32)
+    for b in range(OWN):
+        sum_l = w * sum_l + p1r[b, 0].astype(F32)
+        sum_d = w * sum_d + p1r[OWN - 1 - b, 1].astype(F32)
+    p2s[0] = sum_l.astype(BF16)
+    p2s[1] = sum_d.astype(BF16)
+
+    col = sup // 2
+    half = sup % 2
+    ncol = nsb // 2
+
+    def col_copy(j, slot):
+        other = (col + j) % ncol
+        later = (other > col).astype(jnp.int32)
+        return pltpu.make_async_remote_copy(
+            src_ref=p2s.at[1 - later], dst_ref=p2r.at[slot], send_sem=s2.at[other], recv_sem=r2.at[slot],
+            device_id=((other * 2 + half) * OWN + own, ch), device_id_type=MESH,
+        )
+
+    def half_copy():
+        return pltpu.make_async_remote_copy(
+            src_ref=swap_s, dst_ref=swap_r, send_sem=sh.at[0], recv_sem=sh.at[1],
+            device_id=((col * 2 + 1 - half) * OWN + own, ch), device_id_type=MESH,
+        )
+
+    @pl.loop(1, ncol)
+    def _(j):
+        col_copy(j, col).start()
+
+    scale = dot(
+        -lam_own * res_own, ((iota((POLES, BLK), 1) // 16) == iota((POLES, BLK), 0)).astype(F32), precision=HIGHEST
+    )
+    scale_row = jnp.sum(jnp.where(diag, scale, 0.0), axis=0, keepdims=True)
+
+    @pl.loop(0, ncol)
+    def _(b):
+        gap = jnp.maximum(jnp.abs(col - b) - 1, 0).astype(F32) * float(TOK * OWN * 2)
+        coef_s[b] = jnp.exp(-lam_pc * gap)
+
+    wide_w = jnp.exp(-float(TOK * OWN) * lam_pc)
+    wide_w2 = jnp.exp(-float(TOK * OWN * 2) * lam_pc)
+
+    place_s[...] = (
+        (iota((OWN * BLK, TOK), 0) // BLK == iota((OWN * BLK, TOK), 1) // 16)
+        & (iota((OWN * BLK, TOK), 0) % 16 == iota((OWN * BLK, TOK), 1) % 16)
+    ).astype(BF16)
+    zero = jnp.zeros((POLES, BLK), F32)
+
+    def gather(j, sums):
+        other = (col + j) % ncol
+        col_copy(j, other).wait_recv()
+        term = coef_s[other] * p2r[other].astype(F32)
+        later = other > col
+        return sums[0] + jnp.where(later, 0.0, term), sums[1] + jnp.where(later, term, 0.0)
+
+    col_s, col_f = lax.fori_loop(1, ncol, gather, (zero, zero))
+    swap_s[0] = jnp.where(half == 0, sum_l + wide_w2 * col_s, col_s).astype(BF16)
+    swap_s[1] = jnp.where(half == 0, col_f, sum_d + wide_w2 * col_f).astype(BF16)
+    half_copy().start()
 
     @pl.loop(0, OWN)
     def _(i):
@@ -205,64 +287,6 @@
     send_own(pbs, pbr, sb_, rb_)
     pbr[own] = pbs[own]
 
-    rows = pl.ds(pl.multiple_of(own * 16, 16), 16)
-    lam_own = lam_s[rows, :]
-    res_own = res_s[rows, :]
-    to_chan = ((iota((16, BLK), 1) // 16) == iota((16, BLK), 0)).astype(F32)
-    lam_pc = dot(lam_own, to_chan, ((0,), (0,)), HIGHEST)
-    res_pc = dot(res_own, to_chan, ((0,), (0,)), HIGHEST)
-    w = jnp.exp(-float(TOK) * lam_pc)
-    e1 = jnp.exp(-lam_pc)
-    re1 = res_pc * e1
-
-    wait_own(p1s, p1r, s1, r1)
-    sum_l = jnp.zeros((POLES, BLK), F32)
-    sum_d = jnp.zeros((POLES, BLK), F32)
-    for b in range(OWN):
-        sum_l = w * sum_l + p1r[b, 0].astype(F32)
-        sum_d = w * sum_d + p1r[OWN - 1 - b, 1].astype(F32)
-    p2s[0] = sum_l.astype(BF16)
-    p2s[1] = sum_d.astype(BF16)
-
-    col = sup // 2
-    half = sup % 2
-    ncol = nsb // 2
-
-    def col_copy(j, slot):
-        other = (col + j) % ncol
-        later = (other > col).astype(jnp.int32)
-        return pltpu.make_async_remote_copy(
-            src_ref=p2s.at[1 - later], dst_ref=p2r.at[slot], send_sem=s2.at[other], recv_sem=r2.at[slot],
-            device_id=((other * 2 + half) * OWN + own, ch), device_id_type=MESH,
-        )
-
-    def half_copy():
-        return pltpu.make_async_remote_copy(
-            src_ref=swap_s, dst_ref=swap_r, send_sem=sh.at[0], recv_sem=sh.at[1],
-            device_id=((col * 2 + 1 - half) * OWN + own, ch), device_id_type=MESH,
-        )
-
-    @pl.loop(1, ncol)
-    def _(j):
-        col_copy(j, col).start()
-
-    scale = dot(
-        -lam_own * res_own, ((iota((POLES, BLK), 1) // 16) == iota((POLES, BLK), 0)).astype(F32), precision=HIGHEST
-    )
-    scale_row = jnp.sum(jnp.where(diag, scale, 0.0), axis=0, keepdims=True)
-
-    @pl.loop(0, ncol)
-    def _(b):
-        gap = jnp.maximum(jnp.abs(col - b) - 1, 0).astype(F32) * float(TOK * OWN * 2)
-        coef_s[b] = jnp.exp(-lam_pc * gap)
-
-    wide_w = jnp.exp(-float(TOK * OWN) * lam_pc)
-    wide_w2 = jnp.exp(-float(TOK * OWN * 2) * lam_pc)
-
-    place_s[...] = (
-        (iota((OWN * BLK, TOK), 0) // BLK == iota((OWN * BLK, TOK), 1) // 16)
-        & (iota((OWN * BLK, TOK), 0) % 16 == iota((OWN * BLK, TOK), 1) % 16)
-    ).astype(BF16)
     @pl.loop(0, OWN)
     def _(i):
         cols = pl.ds(pl.multiple_of(i * BLK, BLK), BLK)
@@ -275,33 +299,6 @@
             mat = jnp.where(col_t <= row_t, mat, 0.0).astype(BF16)
             acc = jnp.where(lane_group == g, dot(mat, x), acc)
         zl_s[:, cols] = acc
-
-    zero = jnp.zeros((POLES, BLK), F32)
-
-    def gather(j, sums):
-        other = (col + j) % ncol
-        col_copy(j, other).wait_recv()
-        term = coef_s[other] * p2r[other].astype(F32)
-        later = other > col
-        return sums[0] + jnp.where(later, 0.0, term), sums[1] + jnp.where(later, term, 0.0)
-
-    col_s, col_f = lax.fori_loop(1, ncol, gather, (zero, zero))
-    swap_s[0] = jnp.where(half == 0, sum_l + wide_w2 * col_s, col_s).astype(BF16)
-    swap_s[1] = jnp.where(half == 0, col_f, sum_d + wide_w2 * col_f).astype(BF16)
-    half_copy().start()
-
-    @pl.loop(0, OWN)
-    def _(i):
-        cols = pl.ds(pl.multiple_of(i * BLK, BLK), BLK)
-        d = d_s[:, cols]
-        acc = jnp.zeros((TOK, BLK), F32)
-        h = h_s[i]
-        for g in range(16):
-            wide = jnp.broadcast_to(h[g : g + 1, :], (TOK, TOK))
-            mat = pltpu.roll(wide, 0, 1, stride=1, stride_axis=0)
-            mat = jnp.where(col_t >= row_t, mat, 0.0).astype(BF16)
-            acc = jnp.where(lane_group == g, dot(mat, d), acc)
-        fl_s[:, cols] = acc
 
     wait_own(pms, pmr, sm, rm)
     wait_own(pbs, pbr, sb_, rb_)
@@ -362,6 +359,19 @@
     send_own(p3s, p3r, s3, r3)
     p3r[own] = p3s[own]
     p4r[sup] = p4s[...]
+
+    @pl.loop(0, OWN)
+    def _(i):
+        cols = pl.ds(pl.multiple_of(i * BLK, BLK), BLK)
+        d = d_s[:, cols]
+        acc = jnp.zeros((TOK, BLK), F32)
+        h = h_s[i]
+        for g in range(16):
+            wide = jnp.broadcast_to(h[g : g + 1, :], (TOK, TOK))
+            mat = pltpu.roll(wide, 0, 1, stride=1, stride_axis=0)
+            mat = jnp.where(col_t >= row_t, mat, 0.0).astype(BF16)
+            acc = jnp.where(lane_group == g, dot(mat, d), acc)
+        fl_s[:, cols] = acc
 
     @pl.loop(0, OWN)
     def _(j):

time: 57.4 us -> 56.4 us (0.983)
  Pallas kernels: 56.6 us -> 55.7 us
    pallas_call x1, Pallas kernels: 55.4 us -> 54.4 us  [exchange(): pl.pallas_call(functools.partial(comm_kernel, nsb, nch), out_shape=(*[jax...]
where the time goes in v4:
time: 56.4 us; the launch traced here: 56.3 us
  Pallas kernels  55.7 us (99%)
  between operations  0.64 us (1%)
    pallas_call x1, Pallas kernels, exchange(): pl.pallas_call(functools.partial(comm_kernel, nsb, nch), out_shape=(*[jax...  54.4 us
    pallas_call x1, Pallas kernels, store(): pl.pallas_call(store_kernel, out_shape=tuple((jax.ShapeDtypeStruct(val.sh...  1.21 us

profile of v4, /device:TPU:1, one launch (start us, length us, event | category | flops | bytes accessed | tf_op | source)
XLA Modules:
  0.0 56.3 jit_solution(16787771530458121290)
XLA Ops:
  0.6 54.4 %exchange.1 = (bf16[128,2048]{1,0:T(8,128)(2,1)S(1)}, bf16[128,2048]{1,0:T(8,128)(2,1)S(1)}, bf16[128,2048]{1,0:T(8,128)(2,1)S(1)}, f32[16,512]{1,0:T(8,128)S(1)...) custom-call(bf16[128,2048]{1,0:T(8,128)(2,1)} %q_hbm.1, bf16[128,2048]{1,0:T(8,128)(2,1)} %k_hbm.1, ...), custom_call_target="tpu_custom_call" | custom-call | tf_op jit(solution)/shard_map/exchange/pallas_call | solution.py:472
  55.1 1.2 %store.1 = (bf16[128,2048]{1,0:T(8,128)(2,1)}, bf16[128,2048]{1,0:T(8,128)(2,1)}, bf16[128,2048]{1,0:T(8,128)(2,1)}, f32[16,512]{1,0:T(8,128)}, f32[16,512]{1,0:T(8,128)}, /*index=5*/f32[1,8192]{1,0:T(1,128)}) custom-call(bf16[128,2048]{1,0:T(8,128)(2,1)S(1)} %get-tuple-element.18.refs_0_, bf16[128,2048]{1,0:T(8,128)(2,1)S(1)} %get-tuple-element.19.refs_1_, ...), custom_call_target="tpu_custom_call" | custom-call | tf_op jit(solution)/shard_map/store/pallas_call | solution.py:545

commit v5 on v4

--- a/solution.py
+++ b/solution.py
@@ -43,6 +43,11 @@
     ch = lax.axis_index("ch")
     own = ctx % OWN
     sup = ctx // OWN
+    col = sup // 2
+    half = sup % 2
+    ncol = nsb // 2
+    plane = 2 * nch * OWN
+    here = (half * nch + ch) * OWN + own
 
     def load(i, n):
         cols = pl.ds(pl.multiple_of(i * BLK, BLK), BLK)
@@ -69,19 +74,14 @@
     def greet(ctx_to, ch_to):
         pl.semaphore_signal(barrier, inc=1, device_id=(ctx_to, ch_to), device_id_type=MESH)
 
-    @pl.loop(1, OWN)
-    def _(j):
-        greet(sup * OWN + (own + j) % OWN, ch)
-
-    @pl.loop(1, nsb)
-    def _(j):
-        greet(((sup + j) % nsb) * OWN + own, ch)
-
-    @pl.loop(1, nch)
-    def _(i):
-        @pl.loop(0, OWN)
-        def _(j):
-            greet(sup * OWN + j, (ch + i) % nch)
+    @pl.loop(1, plane)
+    def _(n):
+        there = (here + n) % plane
+        greet((col * 2 + there // (nch * OWN)) * OWN + there % OWN, (there // OWN) % nch)
+
+    @pl.loop(1, ncol)
+    def _(j):
+        greet((((col + j) % ncol) * 2 + half) * OWN + own, ch)
 
     lane_t = iota((GROUP, TOK), 1).astype(F32)
     same_group = (iota((BLK, BLK), 0) % 16) == (iota((BLK, BLK), 1) // 16)
@@ -116,7 +116,7 @@
             full = jnp.where(same_group, dot(table[i], val), 0.0).astype(BF16)
             p1s[i, n] = dot(pick_pole, full).astype(BF16)
 
-    pl.semaphore_wait(barrier, (OWN - 1) + (nsb - 1) + (nch - 1) * OWN)
+    pl.semaphore_wait(barrier, (plane - 1) + (ncol - 1))
 
     def to_own(j, src, dst, send, recv):
         other = (own + j) % OWN
@@ -188,6 +188,19 @@
     diag = (lane_row % 16) == iota((16, BLK), 0)
     flip = (row_t == TOK - 1 - col_t).astype(BF16)
 
+    @pl.loop(0, OWN)
+    def _(i):
+        cols = pl.ds(pl.multiple_of(i * BLK, BLK), BLK)
+        x = x_s[:, cols]
+        acc = jnp.zeros((TOK, BLK), F32)
+        hr = hr_s[i]
+        for g in range(16):
+            wide = jnp.broadcast_to(hr[g : g + 1, :], (TOK, TOK))
+            mat = pltpu.roll(wide, 0, 1, stride=1, stride_axis=0)
+            mat = jnp.where(col_t <= row_t, mat, 0.0).astype(BF16)
+            acc = jnp.where(lane_group == g, dot(mat, x), acc)
+        zl_s[:, cols] = acc
+
     rows = pl.ds(pl.multiple_of(own * 16, 16), 16)
     lam_own = lam_s[rows, :]
     res_own = res_s[rows, :]
@@ -207,9 +220,6 @@
     p2s[0] = sum_l.astype(BF16)
     p2s[1] = sum_d.astype(BF16)
 
-    col = sup // 2
-    half = sup % 2
-    ncol = nsb // 2
 
     def col_copy(j, slot):
         other = (col + j) % ncol
@@ -290,15 +300,15 @@
     @pl.loop(0, OWN)
     def _(i):
         cols = pl.ds(pl.multiple_of(i * BLK, BLK), BLK)
-        x = x_s[:, cols]
+        d = d_s[:, cols]
         acc = jnp.zeros((TOK, BLK), F32)
-        hr = hr_s[i]
+        h = h_s[i]
         for g in range(16):
-            wide = jnp.broadcast_to(hr[g : g + 1, :], (TOK, TOK))
+            wide = jnp.broadcast_to(h[g : g + 1, :], (TOK, TOK))
             mat = pltpu.roll(wide, 0, 1, stride=1, stride_axis=0)
-            mat = jnp.where(col_t <= row_t, mat, 0.0).astype(BF16)
-            acc = jnp.where(lane_group == g, dot(mat, x), acc)
-        zl_s[:, cols] = acc
+            mat = jnp.where(col_t >= row_t, mat, 0.0).astype(BF16)
+            acc = jnp.where(lane_group == g, dot(mat, d), acc)
+        fl_s[:, cols] = acc
 
     wait_own(pms, pmr, sm, rm)
     wait_own(pbs, pbr, sb_, rb_)
@@ -346,32 +356,44 @@
     p4s[...] = pack(part[0:1] + r_row, part[1:2] + m_row, part[2:3])
 
     def grad_copy(j, slot):
-        other = (sup + j) % nsb
+        other = (col + j) % ncol
         return pltpu.make_async_remote_copy(
             src_ref=p4s, dst_ref=p4r.at[slot], send_sem=s4.at[other], recv_sem=r4.at[slot],
-            device_id=(other * OWN + own, ch), device_id_type=MESH,
-        )
-
-    @pl.loop(1, nsb)
-    def _(j):
-        grad_copy(j, sup).start()
+            device_id=((other * 2 + half) * OWN + own, ch), device_id_type=MESH,
+        )
+
+    @pl.loop(1, ncol)
+    def _(j):
+        grad_copy(j, col).start()
 
     send_own(p3s, p3r, s3, r3)
     p3r[own] = p3s[own]
-    p4r[sup] = p4s[...]
-
-    @pl.loop(0, OWN)
-    def _(i):
-        cols = pl.ds(pl.multiple_of(i * BLK, BLK), BLK)
-        d = d_s[:, cols]
-        acc = jnp.zeros((TOK, BLK), F32)
-        h = h_s[i]
-        for g in range(16):
-            wide = jnp.broadcast_to(h[g : g + 1, :], (TOK, TOK))
-            mat = pltpu.roll(wide, 0, 1, stride=1, stride_axis=0)
-            mat = jnp.where(col_t >= row_t, mat, 0.0).astype(BF16)
-            acc = jnp.where(lane_group == g, dot(mat, d), acc)
-        fl_s[:, cols] = acc
+    p4r[col] = p4s[...]
+
+    length = float(TOK * OWN * nsb)
+
+    @pl.loop(1, ncol)
+    def _(j):
+        grad_copy(j, (col + j) % ncol).wait_recv()
+
+    total = p4r[0].astype(F32)
+    for b in range(1, ncol):
+        total = total + p4r[b].astype(F32)
+    r_row, m_row, k_row = unpack(total)
+    p5s[...] = pack(r_row / length, m_row * scale_row / math.sqrt(length), k_row / math.sqrt(length))
+
+    def last_copy(n, mine):
+        there = (here + n) % plane
+        slot = here if mine else there
+        return pltpu.make_async_remote_copy(
+            src_ref=p5s, dst_ref=p5r.at[slot], send_sem=s5.at[there], recv_sem=r5.at[slot],
+            device_id=((col * 2 + there // (nch * OWN)) * OWN + there % OWN, (there // OWN) % nch),
+            device_id_type=MESH,
+        )
+
+    for n in range(1, plane):
+        last_copy(n, True).start()
+    p5r[here] = p5s[...]
 
     @pl.loop(0, OWN)
     def _(j):
@@ -395,35 +417,6 @@
         gk_ref[:, cols] = (flow * v_ref[:, cols].astype(F32)).astype(BF16)
         gv_ref[:, cols] = (flow * k_ref[:, cols].astype(F32)).astype(BF16)
 
-    length = float(TOK * OWN * nsb)
-
-    @pl.loop(1, nsb)
-    def _(j):
-        grad_copy(j, (sup + j) % nsb).wait_recv()
-
-    total = p4r[0].astype(F32)
-    for b in range(1, nsb):
-        total = total + p4r[b].astype(F32)
-    r_row, m_row, k_row = unpack(total)
-    p5s[...] = pack(r_row / length, m_row * scale_row / math.sqrt(length), k_row / math.sqrt(length))
-
-    def last_copy(i, j, mine):
-        ch_to = (ch + i) % nch
-        own_to = (own + j) % OWN
-        here = ch * OWN + own
-        there = ch_to * OWN + own_to
-        slot = here if mine else there
-        return pltpu.make_async_remote_copy(
-            src_ref=p5s, dst_ref=p5r.at[slot], send_sem=s5.at[there], recv_sem=r5.at[slot],
-            device_id=(sup * OWN + own_to, ch_to), device_id_type=MESH,
-        )
-
-    @pl.loop(1, nch * OWN)
-    def _(n):
-        last_copy(n // OWN, n % OWN, True).start()
-
-    p5r[ch * OWN + own] = p5s[...]
-
     sent_own(p1s, p1r, s1, r1)
     sent_own(pms, pmr, sm, rm)
     sent_own(pbs, pbr, sb_, rb_)
@@ -435,21 +428,23 @@
     def _(j):
         col_copy(j, col).wait_send()
 
-    @pl.loop(1, nsb)
-    def _(j):
-        grad_copy(j, sup).wait_send()
-
-    @pl.loop(1, nch * OWN)
+    @pl.loop(1, ncol)
+    def _(j):
+        grad_copy(j, col).wait_send()
+
+    @pl.loop(1, plane)
     def _(n):
-        last_copy(n // OWN, n % OWN, False).wait_recv()
-
-    @pl.loop(1, nch * OWN)
+        last_copy(n, True).wait_send()
+
+    @pl.loop(1, plane)
     def _(n):
-        last_copy(n // OWN, n % OWN, True).wait_send()
+        last_copy(n, False).wait_recv()
 
     keep = (iota((POLES, OWN * BLK), 1) % BLK) // 16 == iota((POLES, OWN * BLK), 0)
     for i in range(nch):
-        rows = [unpack(p5r[i * OWN + j].astype(F32)) for j in range(OWN)]
+        rows = [
+            unpack(p5r[i * OWN + j].astype(F32) + p5r[(nch + i) * OWN + j].astype(F32)) for j in range(OWN)
+        ]
         parts = []
         for n in range(2):
             row = jnp.concatenate([val[n] for val in rows], axis=1)
@@ -502,9 +497,9 @@
             pltpu.VMEM((OWN, 4, BLK), F32),
             pltpu.VMEM((OWN, 4, BLK), F32),
             pltpu.VMEM((2, 3 * BLK // 2), BF16),
-            pltpu.VMEM((nsb, 2, 3 * BLK // 2), BF16),
+            pltpu.VMEM((nsb // 2, 2, 3 * BLK // 2), BF16),
             pltpu.VMEM((2, 3 * BLK // 2), BF16),
-            pltpu.VMEM((nch * OWN, 2, 3 * BLK // 2), BF16),
+            pltpu.VMEM((2 * nch * OWN, 2, 3 * BLK // 2), BF16),
             pltpu.VMEM((nsb // 2,) + state, F32),
             pltpu.VMEM((OWN * BLK, TOK), BF16),
             pltpu.VMEM((2,) + state, BF16),
@@ -515,8 +510,8 @@
             dma((nsb // 2,)), dma((nsb // 2,)),
             dma((OWN,)), dma((OWN,)),
             dma((OWN,)), dma((OWN,)),
-            dma((nsb,)), dma((nsb,)),
-            dma((nch * OWN,)), dma((nch * OWN,)),
+            dma((nsb // 2,)), dma((nsb // 2,)),
+            dma((2 * nch * OWN,)), dma((2 * nch * OWN,)),
         ],
         compiler_params=pltpu.CompilerParams(
             collective_id=0, has_side_effects=True, vmem_limit_bytes=48 << 20

time: 56.4 us -> 58.3 us (1.034)
  Pallas kernels: 55.7 us -> 57.5 us
    pallas_call x1, Pallas kernels: 54.4 us -> 56.3 us  [exchange(): pl.pallas_call(functools.partial(comm_kernel, nsb, nch), out_shape=(*[jax...]
where the time goes in v5:
time: 58.3 us; the launch traced here: 58.2 us
  Pallas kernels  57.5 us (99%)
  between operations  0.64 us (1%)
    pallas_call x1, Pallas kernels, exchange(): pl.pallas_call(functools.partial(comm_kernel, nsb, nch), out_shape=(*[jax...  56.3 us
    pallas_call x1, Pallas kernels, store(): pl.pallas_call(store_kernel, out_shape=tuple((jax.ShapeDtypeStruct(val.sh...  1.21 us

profile of v5, /device:TPU:1, one launch (start us, length us, event | category | flops | bytes accessed | tf_op | source)
XLA Modules:
  0.0 58.2 jit_solution(12451720325488575158)
XLA Ops:
  0.6 56.3 %exchange.1 = (bf16[128,2048]{1,0:T(8,128)(2,1)S(1)}, bf16[128,2048]{1,0:T(8,128)(2,1)S(1)}, bf16[128,2048]{1,0:T(8,128)(2,1)S(1)}, f32[16,512]{1,0:T(8,128)S(1)...) custom-call(bf16[128,2048]{1,0:T(8,128)(2,1)} %q_hbm.1, bf16[128,2048]{1,0:T(8,128)(2,1)} %k_hbm.1, ...), custom_call_target="tpu_custom_call" | custom-call | tf_op jit(solution)/shard_map/exchange/pallas_call | solution.py:467
  57.0 1.2 %store.1 = (bf16[128,2048]{1,0:T(8,128)(2,1)}, bf16[128,2048]{1,0:T(8,128)(2,1)}, bf16[128,2048]{1,0:T(8,128)(2,1)}, f32[16,512]{1,0:T(8,128)}, f32[16,512]{1,0:T(8,128)}, /*index=5*/f32[1,8192]{1,0:T(1,128)}) custom-call(bf16[128,2048]{1,0:T(8,128)(2,1)S(1)} %get-tuple-element.18.refs_0_, bf16[128,2048]{1,0:T(8,128)(2,1)S(1)} %get-tuple-element.19.refs_1_, ...), custom_call_target="tpu_custom_call" | custom-call | tf_op jit(solution)/shard_map/store/pallas_call | solution.py:540

commit v6 on v5

--- a/solution.py
+++ b/solution.py
@@ -150,36 +150,6 @@
     send_own(p1s, p1r, s1, r1)
     p1r[own] = p1s[own]
 
-    @pl.loop(0, OWN)
-    def _(i):
-        rows = pl.ds(pl.multiple_of(i * 16, 16), 16)
-        cols = pl.ds(pl.multiple_of(i * BLK, BLK), BLK)
-        lam = lam_s[rows, :]
-        res = res_s[rows, :]
-        taps = jnp.zeros((GROUP, TOK), F32)
-        back = jnp.zeros((GROUP, TOK), F32)
-        for p in range(POLES):
-            lam_p = lam[:, p : p + 1]
-            res_p = res[:, p : p + 1]
-            ed = jnp.exp(-lam_p * lane_t)
-            el = jnp.exp(-lam_p * (TOK - 1.0 - lane_t))
-            at = pl.ds(p * 16, 16)
-            ed2_s[i, at, :] = (ed * (lane_t + 1.0)).astype(BF16)
-            el2_s[i, at, :] = (el * (TOK - 1.0 - lane_t)).astype(BF16)
-            taps = taps + res_p * ed
-            back = back + (res_p * jnp.exp(-lam_p)) * el
-        h_s[i] = taps
-        hr_s[i] = jnp.where(lane_t == 0.0, taps, back)
-        x = x_s[:, cols]
-        d = d_s[:, cols]
-        pbs[i, 2:3, :] = jnp.sum(x.astype(F32) * d.astype(F32), axis=0, keepdims=True)
-        for n, (table, val) in enumerate(((el2_s, x), (ed2_s, d))):
-            full = jnp.where(same_group, dot(table[i], val), 0.0).astype(BF16)
-            pms[i, n] = dot(pick_pole, full).astype(BF16)
-
-    send_own(pms, pmr, sm, rm)
-    pmr[own] = pms[own]
-
     row_t = iota((TOK, TOK), 0)
     col_t = iota((TOK, TOK), 1)
     lane_group = iota((TOK, BLK), 1) // 16
@@ -191,90 +161,12 @@
     @pl.loop(0, OWN)
     def _(i):
         cols = pl.ds(pl.multiple_of(i * BLK, BLK), BLK)
-        x = x_s[:, cols]
-        acc = jnp.zeros((TOK, BLK), F32)
-        hr = hr_s[i]
-        for g in range(16):
-            wide = jnp.broadcast_to(hr[g : g + 1, :], (TOK, TOK))
-            mat = pltpu.roll(wide, 0, 1, stride=1, stride_axis=0)
-            mat = jnp.where(col_t <= row_t, mat, 0.0).astype(BF16)
-            acc = jnp.where(lane_group == g, dot(mat, x), acc)
-        zl_s[:, cols] = acc
-
-    rows = pl.ds(pl.multiple_of(own * 16, 16), 16)
-    lam_own = lam_s[rows, :]
-    res_own = res_s[rows, :]
-    to_chan = ((iota((16, BLK), 1) // 16) == iota((16, BLK), 0)).astype(F32)
-    lam_pc = dot(lam_own, to_chan, ((0,), (0,)), HIGHEST)
-    res_pc = dot(res_own, to_chan, ((0,), (0,)), HIGHEST)
-    w = jnp.exp(-float(TOK) * lam_pc)
-    e1 = jnp.exp(-lam_pc)
-    re1 = res_pc * e1
-
-    wait_own(p1s, p1r, s1, r1)
-    sum_l = jnp.zeros((POLES, BLK), F32)
-    sum_d = jnp.zeros((POLES, BLK), F32)
-    for b in range(OWN):
-        sum_l = w * sum_l + p1r[b, 0].astype(F32)
-        sum_d = w * sum_d + p1r[OWN - 1 - b, 1].astype(F32)
-    p2s[0] = sum_l.astype(BF16)
-    p2s[1] = sum_d.astype(BF16)
-
-
-    def col_copy(j, slot):
-        other = (col + j) % ncol
-        later = (other > col).astype(jnp.int32)
-        return pltpu.make_async_remote_copy(
-            src_ref=p2s.at[1 - later], dst_ref=p2r.at[slot], send_sem=s2.at[other], recv_sem=r2.at[slot],
-            device_id=((other * 2 + half) * OWN + own, ch), device_id_type=MESH,
-        )
-
-    def half_copy():
-        return pltpu.make_async_remote_copy(
-            src_ref=swap_s, dst_ref=swap_r, send_sem=sh.at[0], recv_sem=sh.at[1],
-            device_id=((col * 2 + 1 - half) * OWN + own, ch), device_id_type=MESH,
-        )
-
-    @pl.loop(1, ncol)
-    def _(j):
-        col_copy(j, col).start()
-
-    scale = dot(
-        -lam_own * res_own, ((iota((POLES, BLK), 1) // 16) == iota((POLES, BLK), 0)).astype(F32), precision=HIGHEST
-    )
-    scale_row = jnp.sum(jnp.where(diag, scale, 0.0), axis=0, keepdims=True)
-
-    @pl.loop(0, ncol)
-    def _(b):
-        gap = jnp.maximum(jnp.abs(col - b) - 1, 0).astype(F32) * float(TOK * OWN * 2)
-        coef_s[b] = jnp.exp(-lam_pc * gap)
-
-    wide_w = jnp.exp(-float(TOK * OWN) * lam_pc)
-    wide_w2 = jnp.exp(-float(TOK * OWN * 2) * lam_pc)
-
-    place_s[...] = (
-        (iota((OWN * BLK, TOK), 0) // BLK == iota((OWN * BLK, TOK), 1) // 16)
-        & (iota((OWN * BLK, TOK), 0) % 16 == iota((OWN * BLK, TOK), 1) % 16)
-    ).astype(BF16)
-    zero = jnp.zeros((POLES, BLK), F32)
-
-    def gather(j, sums):
-        other = (col + j) % ncol
-        col_copy(j, other).wait_recv()
-        term = coef_s[other] * p2r[other].astype(F32)
-        later = other > col
-        return sums[0] + jnp.where(later, 0.0, term), sums[1] + jnp.where(later, term, 0.0)
-
-    col_s, col_f = lax.fori_loop(1, ncol, gather, (zero, zero))
-    swap_s[0] = jnp.where(half == 0, sum_l + wide_w2 * col_s, col_s).astype(BF16)
-    swap_s[1] = jnp.where(half == 0, col_f, sum_d + wide_w2 * col_f).astype(BF16)
-    half_copy().start()
-
-    @pl.loop(0, OWN)
-    def _(i):
-        cols = pl.ds(pl.multiple_of(i * BLK, BLK), BLK)
         x = dot(flip, x_s[:, cols]).astype(BF16)
         d = d_s[:, cols]
+        pbs[i, 2:3, :] = jnp.sum(x_s[:, cols].astype(F32) * d.astype(F32), axis=0, keepdims=True)
+        lam = lam_s[pl.ds(pl.multiple_of(i * 16, 16), 16), :]
+        for p in range(POLES):
+            ed2_s[i, pl.ds(p * 16, 16), :] = (jnp.exp(-lam[:, p : p + 1] * lane_t) * (lane_t + 1.0)).astype(BF16)
         sums = []
         for g in range(16):
             dm = jnp.where(lane_group == g, d, jnp.zeros_like(d))
@@ -297,18 +189,115 @@
     send_own(pbs, pbr, sb_, rb_)
     pbr[own] = pbs[own]
 
-    @pl.loop(0, OWN)
-    def _(i):
-        cols = pl.ds(pl.multiple_of(i * BLK, BLK), BLK)
+    rows = pl.ds(pl.multiple_of(own * 16, 16), 16)
+    lam_own = lam_s[rows, :]
+    res_own = res_s[rows, :]
+    to_chan = ((iota((16, BLK), 1) // 16) == iota((16, BLK), 0)).astype(F32)
+    lam_pc = dot(lam_own, to_chan, ((0,), (0,)), HIGHEST)
+    res_pc = dot(res_own, to_chan, ((0,), (0,)), HIGHEST)
+    w = jnp.exp(-float(TOK) * lam_pc)
+    e1 = jnp.exp(-lam_pc)
+    re1 = res_pc * e1
+
+    wait_own(p1s, p1r, s1, r1)
+    sum_l = jnp.zeros((POLES, BLK), F32)
+    sum_d = jnp.zeros((POLES, BLK), F32)
+    for b in range(OWN):
+        sum_l = w * sum_l + p1r[b, 0].astype(F32)
+        sum_d = w * sum_d + p1r[OWN - 1 - b, 1].astype(F32)
+    p2s[0] = sum_l.astype(BF16)
+    p2s[1] = sum_d.astype(BF16)
+
+
+    def col_copy(j, slot):
+        other = (col + j) % ncol
+        later = (other > col).astype(jnp.int32)
+        return pltpu.make_async_remote_copy(
+            src_ref=p2s.at[1 - later], dst_ref=p2r.at[slot], send_sem=s2.at[other], recv_sem=r2.at[slot],
+            device_id=((other * 2 + half) * OWN + own, ch), device_id_type=MESH,
+        )
+
+    def half_copy():
+        return pltpu.make_async_remote_copy(
+            src_ref=swap_s, dst_ref=swap_r, send_sem=sh.at[0], recv_sem=sh.at[1],
+            device_id=((col * 2 + 1 - half) * OWN + own, ch), device_id_type=MESH,
+        )
+
+    @pl.loop(1, ncol)
+    def _(j):
+        col_copy(j, col).start()
+
+    scale = dot(
+        -lam_own * res_own, ((iota((POLES, BLK), 1) // 16) == iota((POLES, BLK), 0)).astype(F32), precision=HIGHEST
+    )
+    scale_row = jnp.sum(jnp.where(diag, scale, 0.0), axis=0, keepdims=True)
+
+    @pl.loop(0, ncol)
+    def _(b):
+        gap = jnp.maximum(jnp.abs(col - b) - 1, 0).astype(F32) * float(TOK * OWN * 2)
+        coef_s[b] = jnp.exp(-lam_pc * gap)
+
+    wide_w = jnp.exp(-float(TOK * OWN) * lam_pc)
+    wide_w2 = jnp.exp(-float(TOK * OWN * 2) * lam_pc)
+
+    place_s[...] = (
+        (iota((OWN * BLK, TOK), 0) // BLK == iota((OWN * BLK, TOK), 1) // 16)
+        & (iota((OWN * BLK, TOK), 0) % 16 == iota((OWN * BLK, TOK), 1) % 16)
+    ).astype(BF16)
+    @pl.loop(0, OWN)
+    def _(i):
+        rows = pl.ds(pl.multiple_of(i * 16, 16), 16)
+        cols = pl.ds(pl.multiple_of(i * BLK, BLK), BLK)
+        lam = lam_s[rows, :]
+        res = res_s[rows, :]
+        taps = jnp.zeros((GROUP, TOK), F32)
+        back = jnp.zeros((GROUP, TOK), F32)
+        for p in range(POLES):
+            lam_p = lam[:, p : p + 1]
+            res_p = res[:, p : p + 1]
+            ed = jnp.exp(-lam_p * lane_t)
+            el = jnp.exp(-lam_p * (TOK - 1.0 - lane_t))
+            at = pl.ds(p * 16, 16)
+            el2_s[i, at, :] = (el * (TOK - 1.0 - lane_t)).astype(BF16)
+            taps = taps + res_p * ed
+            back = back + (res_p * jnp.exp(-lam_p)) * el
+        h_s[i] = taps
+        hr_s[i] = jnp.where(lane_t == 0.0, taps, back)
+        x = x_s[:, cols]
         d = d_s[:, cols]
+        for n, (table, val) in enumerate(((el2_s, x), (ed2_s, d))):
+            full = jnp.where(same_group, dot(table[i], val), 0.0).astype(BF16)
+            pms[i, n] = dot(pick_pole, full).astype(BF16)
+
+    send_own(pms, pmr, sm, rm)
+    pmr[own] = pms[own]
+
+    zero = jnp.zeros((POLES, BLK), F32)
+
+    def gather(j, sums):
+        other = (col + j) % ncol
+        col_copy(j, other).wait_recv()
+        term = coef_s[other] * p2r[other].astype(F32)
+        later = other > col
+        return sums[0] + jnp.where(later, 0.0, term), sums[1] + jnp.where(later, term, 0.0)
+
+    col_s, col_f = lax.fori_loop(1, ncol, gather, (zero, zero))
+    swap_s[0] = jnp.where(half == 0, sum_l + wide_w2 * col_s, col_s).astype(BF16)
+    swap_s[1] = jnp.where(half == 0, col_f, sum_d + wide_w2 * col_f).astype(BF16)
+    half_copy().start()
+
+    @pl.loop(0, OWN)
+    def _(i):
+        cols = pl.ds(pl.multiple_of(i * BLK, BLK), BLK)
+        x = x_s[:, cols]
         acc = jnp.zeros((TOK, BLK), F32)
-        h = h_s[i]
+        hr = hr_s[i]
         for g in range(16):
-            wide = jnp.broadcast_to(h[g : g + 1, :], (TOK, TOK))
+            wide = jnp.broadcast_to(hr[g : g + 1, :], (TOK, TOK))
             mat = pltpu.roll(wide, 0, 1, stride=1, stride_axis=0)
-            mat = jnp.where(col_t >= row_t, mat, 0.0).astype(BF16)
-            acc = jnp.where(lane_group == g, dot(mat, d), acc)
-        fl_s[:, cols] = acc
+            mat = jnp.where(col_t <= row_t, mat, 0.0).astype(BF16)
+            acc = jnp.where(lane_group == g, dot(mat, x), acc)
+        zl_s[:, cols] = acc
 
     wait_own(pms, pmr, sm, rm)
     wait_own(pbs, pbr, sb_, rb_)
@@ -394,6 +383,19 @@
     for n in range(1, plane):
         last_copy(n, True).start()
     p5r[here] = p5s[...]
+
+    @pl.loop(0, OWN)
+    def _(i):
+        cols = pl.ds(pl.multiple_of(i * BLK, BLK), BLK)
+        d = d_s[:, cols]
+        acc = jnp.zeros((TOK, BLK), F32)
+        h = h_s[i]
+        for g in range(16):
+            wide = jnp.broadcast_to(h[g : g + 1, :], (TOK, TOK))
+            mat = pltpu.roll(wide, 0, 1, stride=1, stride_axis=0)
+            mat = jnp.where(col_t >= row_t, mat, 0.0).astype(BF16)
+            acc = jnp.where(lane_group == g, dot(mat, d), acc)
+        fl_s[:, cols] = acc
 
     @pl.loop(0, OWN)
     def _(j):

time: 58.3 us -> 55.2 us (0.947)
  the two profiles are of different devices: /device:TPU:1 before, /device:TPU:2 now
where the time goes in v6:
time: 55.2 us; the launch traced here: 55.1 us
  Pallas kernels  54.4 us (99%)
  between operations  0.64 us (1%)
    pallas_call x1, Pallas kernels, exchange(): pl.pallas_call(functools.partial(comm_kernel, nsb, nch), out_shape=(*[jax...  53.2 us
    pallas_call x1, Pallas kernels, store(): pl.pallas_call(store_kernel, out_shape=tuple((jax.ShapeDtypeStruct(val.sh...  1.21 us

profile of v6, /device:TPU:2, one launch (start us, length us, event | category | flops | bytes accessed | tf_op | source)
XLA Modules:
  0.0 55.1 jit_solution(7576738686371304242)
XLA Ops:
  0.6 53.2 %exchange.1 = (bf16[128,2048]{1,0:T(8,128)(2,1)S(1)}, bf16[128,2048]{1,0:T(8,128)(2,1)S(1)}, bf16[128,2048]{1,0:T(8,128)(2,1)S(1)}, f32[16,512]{1,0:T(8,128)S(1)...) custom-call(bf16[128,2048]{1,0:T(8,128)(2,1)} %q_hbm.1, bf16[128,2048]{1,0:T(8,128)(2,1)} %k_hbm.1, ...), custom_call_target="tpu_custom_call" | custom-call | tf_op jit(solution)/shard_map/exchange/pallas_call | solution.py:469
  53.9 1.2 %store.1 = (bf16[128,2048]{1,0:T(8,128)(2,1)}, bf16[128,2048]{1,0:T(8,128)(2,1)}, bf16[128,2048]{1,0:T(8,128)(2,1)}, f32[16,512]{1,0:T(8,128)}, f32[16,512]{1,0:T(8,128)}, /*index=5*/f32[1,8192]{1,0:T(1,128)}) custom-call(bf16[128,2048]{1,0:T(8,128)(2,1)S(1)} %get-tuple-element.18.refs_0_, bf16[128,2048]{1,0:T(8,128)(2,1)S(1)} %get-tuple-element.19.refs_1_, ...), custom_call_target="tpu_custom_call" | custom-call | tf_op jit(solution)/shard_map/store/pallas_call | solution.py:542
